TPU v7x, 512 devices: a whole 4x4x16 slice. The times are simulated.
512 devices in a mesh: dp: 16 (over y, x), seq: 32 (over z, core).
Axes of the slice: x: 4, y: 4, z: 16, core: 2. Of those that a mesh axis runs over, the one named last changes fastest.
Arguments:
- tokens: bfloat16 [16, 8192, 4096], P('dp', 'seq'), may hold values from -6 to 6
- w_qkv: bfloat16 [4096, 768], P('dp'), may hold values from -0.09375 to 0.09375
- norm_gain: float32 [256], replicated, may hold values from 0.1 to 1.9
- w_out: bfloat16 [256, 4096], P(None, 'dp'), may hold values from -0.375 to 0.375
Outputs:
- mixed: bfloat16 [16, 8192, 4096], P('dp', 'seq')
All inputs are finite; a program needn't handle non-finite values.
Results may differ from a plain program's by a relative error of at most 0.015.
Values may be sent and summed in bfloat16 or wider, within the bound.
A program may use at most 64 MiB of HBM per device.

v0:
```python
import jax
import jax.numpy as jnp
from jax import lax
from jax.sharding import PartitionSpec as P

HEAD = 128


def shards(tokens, w_qkv, norm_gain, w_out):
    inputs = tokens[0]
    tok_rows = inputs.shape[0]
    width3 = w_qkv.shape[1]
    feat = width3 // 3
    heads = norm_gain.shape[0] // HEAD
    proj = jnp.dot(
        inputs, lax.all_gather(w_qkv, "dp", axis=0, tiled=True), preferred_element_type=jnp.float32
    )
    query = jax.nn.silu(proj[:, :feat]).astype(jnp.bfloat16).reshape(tok_rows, heads, HEAD)
    keys = jax.nn.silu(proj[:, feat : 2 * feat]).astype(jnp.bfloat16).reshape(tok_rows, heads, HEAD)
    values = proj[:, 2 * feat :].astype(jnp.bfloat16).reshape(tok_rows, heads, HEAD)
    state = jnp.einsum("thA,thB->hAB", keys, values, preferred_element_type=jnp.float32)
    every_state = lax.all_gather(
        state[None].astype(jnp.bfloat16), "seq", axis=0, tiled=True
    ).astype(jnp.float32)
    blocks = every_state.shape[0]
    weights = (jnp.arange(blocks) < lax.axis_index("seq")).astype(jnp.float32)
    prefix = jnp.einsum("n,nhab->hab", weights, every_state, precision=lax.Precision.HIGHEST)
    prefix = prefix.astype(jnp.bfloat16)
    inter = jnp.einsum("thA,hAB->thB", query, prefix, preferred_element_type=jnp.float32)
    scores = jnp.einsum("thA,shA->hts", query, keys, preferred_element_type=jnp.float32)
    rows = jnp.arange(tok_rows)
    causal = rows[:, None] >= rows[None, :]
    scores = jnp.where(causal[None], scores, 0.0).astype(jnp.bfloat16)
    intra = jnp.einsum("hts,shB->thB", scores, values, preferred_element_type=jnp.float32)
    attended = inter + intra
    meansq = jnp.mean(attended * attended, axis=-1, keepdims=True)
    normed = attended * lax.rsqrt(meansq + 1e-06) * norm_gain.reshape(heads, HEAD)
    normed = normed.astype(jnp.bfloat16).reshape(tok_rows, heads * HEAD)
    mixed = jnp.dot(
        normed, lax.all_gather(w_out, "dp", axis=1, tiled=True), preferred_element_type=jnp.float32
    )
    return mixed.astype(jnp.bfloat16)[None]


def solution(mesh):
    return jax.shard_map(
        shards,
        mesh=mesh,
        in_specs=(P("dp", "seq", None), P("dp", None), P(), P(None, "dp")),
        out_specs=P("dp", "seq", None),
        check_vma=False,
    )
```

profile of v0, /device:TPU:1, one launch (start us, length us, event | category | flops | bytes accessed | tf_op | source)
XLA Modules:
  0.0 242.1 jit_solution(8243178207157146970)
XLA Ops:
  6.5 0.0 copy-start
  6.5 0.0 all-gather.5.cloned.1.call-start
  6.5 0.7 all-gather.5.cloned.1.call-update
  7.3 0.0 all-gather.9.cloned.1.call-start
  7.3 85.1 %all-gather.5.cloned.1.call-done = bf16[4096,768]{1,0:T(8,128)(2,1)} async-done(((bf16[256,768]{1,0:T(8,128)(2,1)}), bf16[4096,768]{1,0:T(8,128)(2,1)}) %all-gather.5.cloned.1.call-update) | async-done | bytes 6291472 | tf_op jit(solution)/shard_map/all_gather | solution.py:16
  92.4 0.0 copy-done
  92.4 4.6 %fusion.1 = f32[256,768]{1,0:T(8,128)S(1)} fusion(bf16[4096,768]{1,0:T(8,128)(2,1)} %all-gather.5.cloned.1.call-done, bf16[1,256,4096]{2,1,0:T(8,128)(2,1)S(1)} %copy-done), kind=kOutput, calls=%fused_computation.2 | convolution fusion | flops 1610612736 | bytes 9175040 | tf_op jit(solution)/shard_map/dot_general | solution.py:15
  96.9 0.1 fusion.13
  97.1 0.1 copy.16
  97.2 0.1 copy.17
  97.3 0.8 convolution_convert_fusion.1
  98.2 0.0 all-gather.9.cloned.1.call-update
  98.2 0.0 copy-start.1
  98.2 0.0 all-gather.7.cloned.1.call-start
  98.2 0.7 all-gather.7.cloned.1.call-update
  99.0 0.4 fusion.6
  99.3 71.0 %all-gather.9.cloned.1.call-done = bf16[64,128,128]{2,1,0:T(8,128)(2,1)} async-done(((bf16[2,128,128]{2,1,0:T(8,128)(2,1)}), bf16[64,128,128]{2,1,0:T(8,128)(2,1)}) %all-gather.9.cloned.1.call-update) | async-done | bytes 2097168 | tf_op jit(solution)/shard_map/all_gather | solution.py:22
  170.3 2.9 %fusion.3 = bf16[1,2,128,128]{3,0,2,1:T(2,128)(2,1)S(1)} fusion(bf16[32,2,128,128]{3,2,1,0:T(8,128)(2,1)} %bitcast.39, s32[]{:T(128)S(6)} %axis_index.12), kind=kOutput, calls=%fused_computation.4 | convolution fusion | flops 2097184 | bytes 2162692 | tf_op jit(solution)/shard_map/n,nhab->hab/dot_general | solution.py:27
  173.2 0.1 copy.15
  173.3 0.2 multiply_reduce_fusion
  173.5 0.0 copy-done.1
  173.6 0.1 multiply_convert_fusion
  173.7 58.3 %all-gather.7.cloned.1.call-done = bf16[256,4096]{1,0:T(8,128)(2,1)} async-done(((bf16[256,256]{1,0:T(8,128)(2,1)}), bf16[256,4096]{1,0:T(8,128)(2,1)}) %all-gather.7.cloned.1.call-update) | async-done | bytes 2097168 | tf_op jit(solution)/shard_map/all_gather | solution.py:40
  231.9 3.6 %fusion = bf16[1,256,4096]{2,1,0:T(8,128)(2,1)} fusion(bf16[256,256]{0,1:T(8,128)(2,1)S(1)} %bitcast.40, bf16[256,4096]{1,0:T(8,128)(2,1)} %all-gather.7.cloned.1.call-done), kind=kOutput, calls=%fused_computation.1 | convolution fusion | flops 537919488 | bytes 4325376 | tf_op jit(solution)/shard_map/dot_general | solution.py:39
  (3 shorter events, 0.0 us)
Async XLA Ops:
  6.5 85.8 %copy-start = (bf16[1,256,4096]{2,1,0:T(8,128)(2,1)S(1)}, bf16[1,256,4096]{2,1,0:T(8,128)(2,1)}, u32[]{:S(2)}) copy-start(bf16[1,256,4096]{2,1,0:T(8,128)(2,1)} %param.4) | copy-start | bytes 6291460
  6.5 85.8 %all-gather.5.cloned.1.call-start = ((), (), s32[]{:S(2)}) async-start(), calls=%async_computation | async-start | bytes 6684672 | tf_op jit(solution)/shard_map/all_gather | solution.py:16
  7.3 163.1 %all-gather.9.cloned.1.call-start = ((), (), s32[]{:S(2)}) async-start(), calls=%async_computation.2 | async-start | bytes 2162688 | tf_op jit(solution)/shard_map/all_gather | solution.py:22
  98.2 75.4 %copy-start.1 = (f32[256]{0:T(256)S(1)}, f32[256]{0:T(256)}, u32[]{:S(2)}) copy-start(f32[256]{0:T(256)} %param.6) | copy-start | bytes 3076
  98.2 133.7 %all-gather.7.cloned.1.call-start = ((), (), s32[]{:S(2)}) async-start(), calls=%async_computation.1 | async-start | bytes 2228224 | tf_op jit(solution)/shard_map/all_gather | solution.py:40
Sparse Core Ops, SparseCore 0:
  10.4 81.9 all-gather.4
  98.3 71.9 all-gather.8
  173.3 58.5 all-gather.6
where the time goes:
time: 242 us
  waiting for transfers between devices  216 us (89%)
  between operations  13.2 us (5%)
  matrix products  12.4 us (5%)
    all_gather x1, waiting for transfers between devices, shards(): lax.all_gather(w_qkv, 'dp', axis=0, tiled=True)  85.1 us
    all_gather x1, waiting for transfers between devices, shards(): lax.all_gather(state[None].astype(jnp.bfloat16), 'seq', axis=0, tiled=True)  71 us
    all_gather x1, waiting for transfers between devices, shards(): lax.all_gather(w_out, 'dp', axis=1, tiled=True)  58.3 us
  transfers between devices with their start and end apart: 3, of which 3 were waited for; matrix products, arithmetic and copies ran while one was open for 2% of the time, Pallas kernels for 0%

commit v1 on v0

v1 whole, which is shorter than its diff:
```python
import functools

import jax
import jax.numpy as jnp
from jax import lax
from jax.experimental import pallas as pl
from jax.experimental.pallas import tpu as pltpu
from jax.sharding import PartitionSpec as P

MESH = pl.DeviceIdType.MESH
BF16, F32 = jnp.bfloat16, jnp.float32
HEAD = 128
SIDE = 4
GROUP = 4
GROUPS = 4
TOK = 256
BLK = 256


def mod4(value):
    return lax.rem(value + 8, 4)


def kernel(
    tok_ref, w_ref, gain_ref, wo_ref, out_ref,
    x_buf, kv, q, wo, k_act, v_act, intra, near, far, total, nrm, nrm_out, out_buf,
    kv_acc, q_act, state,
    load_sem, send_sem, full_sem, half_sem, scan_send, near_sem, far_sem, pair_send, pair_recv, store_sem,
):
    dp, seq = lax.axis_index("dp"), lax.axis_index("seq")
    y, x = lax.div(dp, SIDE), lax.rem(dp, SIDE)
    z, core = lax.div(seq, 2), lax.rem(seq, 2)
    grp, mem = lax.div(z, GROUP), lax.rem(z, GROUP)
    sibling = (dp, z * 2 + (1 - core))
    lane = pl.multiple_of(core * HEAD, HEAD)

    def at_xy(axis, off):
        if axis == 0:
            return (y * SIDE + mod4(x + off), seq)
        return (mod4(y + off) * SIDE + x, seq)

    def at_z(g, m):
        return (dp, (g * GROUP + m) * 2 + core)

    loads = [
        pltpu.make_async_copy(w_ref.at[:, pl.ds(2 * HEAD + lane, HEAD)], kv.at[dp, :, pl.ds(0, HEAD)], load_sem.at[0]),
        pltpu.make_async_copy(w_ref.at[:, pl.ds(4 * HEAD + lane, HEAD)], kv.at[dp, :, pl.ds(HEAD, HEAD)], load_sem.at[1]),
        pltpu.make_async_copy(w_ref.at[:, pl.ds(lane, HEAD)], q.at[dp], load_sem.at[2]),
        pltpu.make_async_copy(wo_ref.at[pl.ds(lane, HEAD)], wo.at[dp, pl.ds(lane, HEAD)], load_sem.at[3]),
        pltpu.make_async_copy(tok_ref, x_buf.at[pl.ds(pl.multiple_of(core * TOK, TOK), TOK)], load_sem.at[4]),
    ]
    for copy in loads:
        copy.start()
    far[...] = jnp.zeros_like(far)

    barrier = pltpu.get_barrier_semaphore()
    partners = [sibling]
    for off in (1, 2, 3):
        partners += [at_xy(0, off), at_xy(1, off), at_z(grp, mod4(mem + off)), at_z(mod4(grp + off), mem)]
    for partner in partners:
        pl.semaphore_signal(barrier, inc=1, device_id=partner, device_id_type=MESH)
    pl.semaphore_wait(barrier, len(partners))

    def piece(s, block, half, sub=None):
        rows = BLK // 2 if s < 2 else HEAD // 2
        start = half * rows
        if s == 2:
            start = start + lane
        if sub is not None:
            start, rows = start + sub * (rows // 2), rows // 2
        start = pl.multiple_of(start, 32) if not isinstance(start, int) else start
        return (kv, q, wo)[s].at[block, pl.ds(start, rows)]

    def block_at(half, first, second):
        dy, dx = (second, first) if half == 0 else (first, second)
        return mod4(y + dy) * SIDE + mod4(x + dx)

    def send_full(s, half, block, axis, off):
        ref = piece(s, block, half)
        pltpu.make_async_remote_copy(
            src_ref=ref, dst_ref=ref, send_sem=send_sem.at[s], recv_sem=full_sem.at[s, half, block],
            device_id=at_xy(axis, off), device_id_type=MESH,
        ).start()

    def wait_full(s, half, block):
        ref = piece(s, block, half)
        pltpu.make_async_copy(ref, ref, full_sem.at[s, half, block]).wait()

    def send_half(s, half, block, sub, axis, off):
        ref = piece(s, block, half, sub)
        pltpu.make_async_remote_copy(
            src_ref=ref, dst_ref=ref, send_sem=send_sem.at[s], recv_sem=half_sem.at[s, half, block, sub],
            device_id=at_xy(axis, off), device_id_type=MESH,
        ).start()

    def wait_half(s, half, block, sub):
        ref = piece(s, block, half, sub)
        pltpu.make_async_copy(ref, ref, half_sem.at[s, half, block, sub]).wait()

    def stage0(s):
        for half in (0, 1):
            for off in (1, -1):
                send_full(s, half, dp, half, off)
        for half in (0, 1):
            send_full(s, half, dp, half, 2)
        for half in (0, 1):
            for off in (1, -1):
                send_full(s, half, dp, 1 - half, off)

    def stage1(s):
        for first in (1, -1, 2):
            for half in (0, 1):
                block = block_at(half, first, 0)
                wait_full(s, half, block)
                for off in (1, -1):
                    send_full(s, half, block, 1 - half, off)

    def stage2(s):
        for first in (0, 1, -1, 2):
            for second in (-1, 1):
                for half in (0, 1):
                    block = block_at(half, first, second)
                    wait_full(s, half, block)
                    send_half(s, half, block, 0 if second == -1 else 1, 1 - half, -second)

    def stage3(s):
        for first in (0, 1, -1, 2):
            for half in (0, 1):
                for sub in (0, 1):
                    wait_half(s, half, block_at(half, first, 2), sub)

    def sent(s):
        ref = (kv.at[pl.ds(0, 15)], q.at[pl.ds(0, 15)], wo.at[pl.ds(0, 15), pl.ds(0, HEAD)])[s]
        pltpu.make_async_copy(ref, ref, send_sem.at[s]).wait()

    loads[0].wait()
    loads[1].wait()
    stage0(0)
    tokens_out = pltpu.make_async_remote_copy(
        src_ref=tok_ref, dst_ref=x_buf.at[pl.ds(pl.multiple_of(core * TOK, TOK), TOK)],
        send_sem=pair_send.at[0], recv_sem=pair_recv.at[0], device_id=sibling, device_id_type=MESH,
    )
    tokens_out.start()
    stage1(0)
    loads[2].wait()
    stage0(1)
    stage2(0)
    stage1(1)
    loads[3].wait()
    stage0(2)
    loads[4].wait()
    tokens_out.wait()
    stage3(0)

    def project(weights, acc):
        wide = weights.shape[-1]
        for part in range(4):
            term = jnp.dot(
                x_buf[:, pl.ds(part * 1024, 1024)],
                weights[pl.ds(part * 4, 4)].reshape(1024, wide),
                preferred_element_type=F32,
            )
            if part == 0:
                acc[...] = term
            else:
                acc[...] += term

    project(kv, kv_acc)
    keys_in = kv_acc[:, :HEAD]
    k_act[...] = (keys_in / (1.0 + jnp.exp(-keys_in))).astype(BF16)
    v_act[...] = kv_acc[:, HEAD:].astype(BF16)
    for b in (0, 1):
        rows = pl.ds(b * TOK, TOK)
        state[b] = lax.dot_general(
            k_act[rows], v_act[rows], (((0,), (0,)), ((), ())), preferred_element_type=F32
        )
    near[mem] = (state[0] + state[1]).astype(BF16)

    for off in (1, 2, 3):
        pltpu.make_async_remote_copy(
            src_ref=near.at[mem], dst_ref=near.at[mem], send_sem=scan_send.at[off - 1], recv_sem=near_sem.at[mem],
            device_id=at_z(grp, mod4(mem + off)), device_id_type=MESH,
        ).start()
    stage2(1)
    stage1(2)
    for off in (1, 2, 3):
        m = mod4(mem + off)
        pltpu.make_async_copy(near.at[m], near.at[m], near_sem.at[m]).wait()
    all_near = [near[m].astype(F32) for m in range(GROUP)]
    total[...] = (all_near[0] + all_near[1] + all_near[2] + all_near[3]).astype(BF16)

    for off in (2, 1, 3):
        g = grp + off

        @pl.when(g < GROUPS)
        def _():
            pltpu.make_async_remote_copy(
                src_ref=total, dst_ref=far.at[grp], send_sem=scan_send.at[2 + off], recv_sem=far_sem.at[grp],
                device_id=at_z(g, mem), device_id_type=MESH,
            ).start()

    prefix = jnp.zeros((HEAD, HEAD), F32)
    for m in range(GROUP - 1):
        prefix = prefix + jnp.where(m < mem, all_near[m], 0.0)

    stage2(2)
    stage3(1)
    project(q, q_act)
    queries = q_act[...]
    q_act[...] = queries / (1.0 + jnp.exp(-queries))
    causal = lax.broadcasted_iota(jnp.int32, (TOK, TOK), 0) >= lax.broadcasted_iota(jnp.int32, (TOK, TOK), 1)
    for b in (0, 1):
        rows = pl.ds(b * TOK, TOK)
        scores = lax.dot_general(
            q_act[rows].astype(BF16), k_act[rows], (((1,), (1,)), ((), ())), preferred_element_type=F32
        )
        scores = jnp.where(causal, scores, 0.0).astype(BF16)
        intra[rows] = jnp.dot(scores, v_act[rows], preferred_element_type=F32)
    stage3(2)
    wo_out = pltpu.make_async_remote_copy(
        src_ref=wo.at[:, pl.ds(lane, HEAD)], dst_ref=wo.at[:, pl.ds(lane, HEAD)],
        send_sem=pair_send.at[1], recv_sem=pair_recv.at[1], device_id=sibling, device_id_type=MESH,
    )
    wo_out.start()
    for s in range(3):
        sent(s)
    for off in (1, 2, 3):
        pltpu.make_async_copy(near.at[0], near.at[0], scan_send.at[off - 1]).wait()

    for g in range(GROUPS - 1):

        @pl.when(g < grp)
        def _():
            pltpu.make_async_copy(far.at[g], far.at[g], far_sem.at[g]).wait()

        prefix = prefix + jnp.where(g < grp, far[g].astype(F32), 0.0)

    gain = gain_ref[pl.ds(core, 1), :]

    def normed(b):
        rows = pl.ds(pl.multiple_of(b * TOK, TOK), TOK)
        before = prefix + jnp.where(b == 1, state[0], 0.0)
        attended = intra[rows] + jnp.dot(
            q_act[rows].astype(BF16), before.astype(BF16), preferred_element_type=F32
        )
        meansq = jnp.mean(attended * attended, axis=-1, keepdims=True)
        return (attended * lax.rsqrt(meansq + 1e-06) * gain).astype(BF16)

    nrm_out[...] = normed(1 - core)
    nrm_copy = pltpu.make_async_remote_copy(
        src_ref=nrm_out, dst_ref=nrm.at[core], send_sem=pair_send.at[2], recv_sem=pair_recv.at[2],
        device_id=sibling, device_id_type=MESH,
    )
    nrm_copy.start()
    nrm[core] = normed(core)
    wo_out.wait()
    nrm_copy.wait()
    lhs = jnp.concatenate([nrm[0], nrm[1]], axis=1)
    stores = []
    for block in range(16):
        columns = pl.ds(block * BLK, BLK)
        out_buf[:, columns] = jnp.dot(lhs, wo[block], preferred_element_type=F32).astype(BF16)
        if block % 2 == 1:
            columns = pl.ds((block - 1) * BLK, 2 * BLK)
            copy = pltpu.make_async_copy(out_buf.at[:, columns], out_ref.at[:, columns], store_sem.at[block // 2])
            copy.start()
            stores.append(copy)
    for off in (1, 2, 3):

        @pl.when(grp + off < GROUPS)
        def _():
            pltpu.make_async_copy(total, total, scan_send.at[2 + off]).wait()

    for copy in stores:
        copy.wait()


def shards(tokens, w_qkv, norm_gain, w_out):
    hbm = pl.BlockSpec(memory_space=pl.ANY)
    dma = pltpu.SemaphoreType.DMA
    width = tokens.shape[2]
    out = pl.pallas_call(
        kernel,
        out_shape=jax.ShapeDtypeStruct((TOK, width), BF16),
        in_specs=[hbm, hbm, pl.BlockSpec(memory_space=pltpu.VMEM), hbm],
        out_specs=hbm,
        scratch_shapes=[
            pltpu.VMEM((2 * TOK, width), BF16),
            pltpu.VMEM((16, BLK, 2 * HEAD), BF16),
            pltpu.VMEM((16, BLK, HEAD), BF16),
            pltpu.VMEM((16, 2 * HEAD, BLK), BF16),
            pltpu.VMEM((2 * TOK, HEAD), BF16),
            pltpu.VMEM((2 * TOK, HEAD), BF16),
            pltpu.VMEM((2 * TOK, HEAD), F32),
            pltpu.VMEM((GROUP, HEAD, HEAD), BF16),
            pltpu.VMEM((GROUPS, HEAD, HEAD), BF16),
            pltpu.VMEM((HEAD, HEAD), BF16),
            pltpu.VMEM((2, TOK, HEAD), BF16),
            pltpu.VMEM((TOK, HEAD), BF16),
            pltpu.VMEM((TOK, width), BF16),
            pltpu.VMEM((2 * TOK, 2 * HEAD), F32),
            pltpu.VMEM((2 * TOK, HEAD), F32),
            pltpu.VMEM((2, HEAD, HEAD), F32),
            dma((5,)),
            dma((3,)),
            dma((3, 2, 16)),
            dma((3, 2, 16, 2)),
            dma((6,)),
            dma((GROUP,)),
            dma((GROUPS,)),
            dma((3,)),
            dma((3,)),
            dma((8,)),
        ],
        compiler_params=pltpu.CompilerParams(
            collective_id=0, has_side_effects=True, vmem_limit_bytes=48 * 1024 * 1024
        ),
        name="attention_layer",
    )(tokens[0], w_qkv, norm_gain.reshape(2, HEAD), w_out)
    return out[None]


def solution(mesh):
    return jax.shard_map(
        shards,
        mesh=mesh,
        in_specs=(P("dp", "seq", None), P("dp", None), P(), P(None, "dp")),
        out_specs=P("dp", "seq", None),
        check_vma=False,
    )
```

time: 242 us -> 59.8 us (0.25)
  waiting for transfers between devices: 216 us -> 0 us
  Pallas kernels: 0 us -> 54.1 us
  between operations: 13.2 us -> 0.01 us
  matrix products: 12.4 us -> 0 us
  local copies, waits for them, and re-layouts: 0.35 us -> 5.49 us
    all_gather x3 -> x0, waiting for transfers between devices: 214 us -> none  [the longest x1 85.1 us: shards(): lax.all_gather(w_qkv, 'dp', axis=0, tiled=True)]
    pallas_call x0 -> x1, Pallas kernels: none -> 54.1 us  [shards(): pl.pallas_call(kernel, out_shape=jax.ShapeDtypeStruct((TOK, width), BF16)...]
    dot_general x6 -> x0, matrix products: 12.4 us -> none  [the longest x1 4.56 us: shards(): jnp.dot(inputs, lax.all_gather(w_qkv, 'dp', axis=0, tiled=True), preferre...]
    unnamed x4 -> x9, local copies, waits for them, and re-layouts: 0.01 us -> 5.49 us
  transfers between devices with their start and end apart: 3 -> 0, of which waited for: 3 -> 0; matrix products, arithmetic and copies ran while one was open for 2% -> 0% of each run, Pallas kernels for 0% -> 0%
where the time goes in v1:
time: 59.8 us; the launch traced here: 59.6 us
  Pallas kernels  54.1 us (90%)
  local copies, waits for them, and re-layouts  5.49 us (9%)
    pallas_call x1, Pallas kernels, shards(): pl.pallas_call(kernel, out_shape=jax.ShapeDtypeStruct((TOK, width), BF16)...  54.1 us
    unnamed x9, local copies, waits for them, and re-layouts  5.49 us

profile of v1, /device:TPU:1, one launch (start us, length us, event | category | flops | bytes accessed | tf_op | source)
XLA Modules:
  0.0 59.6 jit_solution(15592379622357834380)
XLA Ops:
  0.0 0.0 copy-start
  0.0 1.6 %copy-done = bf16[1,256,4096]{2,1,0:T(8,128)(2,1)S(1)} copy-done((bf16[1,256,4096]{2,1,0:T(8,128)(2,1)S(1)}, bf16[1,256,4096]{2,1,0:T(8,128)(2,1)}, u32[]{:S(2)}) %copy-start) | copy-done | bytes 2097176
  1.6 0.0 copy-start.1
  1.6 1.0 %copy-done.1 = bf16[256,768]{1,0:T(8,128)(2,1)S(1)} copy-done((bf16[256,768]{1,0:T(8,128)(2,1)S(1)}, bf16[256,768]{1,0:T(8,128)(2,1)}, u32[]{:S(2)}) %copy-start.1) | copy-done | bytes 393240
  2.6 0.0 copy-start.2
  2.6 0.9 %copy-done.2 = bf16[256,256]{1,0:T(8,128)(2,1)S(1)} copy-done((bf16[256,256]{1,0:T(8,128)(2,1)S(1)}, bf16[256,256]{1,0:T(8,128)(2,1)}, u32[]{:S(2)}) %copy-start.2) | copy-done | bytes 131096
  3.5 0.0 copy-start.3
  3.5 0.7 %copy-done.3 = f32[256]{0:T(256)S(1)} copy-done((f32[256]{0:T(256)S(1)}, f32[256]{0:T(256)}, u32[]{:S(2)}) %copy-start.3) | copy-done | bytes 1048
  4.2 54.1 %attention_layer.1 = bf16[256,4096]{1,0:T(8,128)(2,1)S(1)} custom-call(bf16[256,4096]{1,0:T(8,128)(2,1)S(1)} %bitcast.4, bf16[256,768]{1,0:T(8,128)(2,1)S(1)} %copy-done.1, f32[2,128]{1,0:T(2,128)S(1)} %bitcast.5, bf16[256,256]{1,0:T(8,128)(2,1)S(1)} %copy-done.2), custom_call_target="tpu_custom_call" | custom-call | tf_op jit(solution)/shard_map/attention_layer/pallas_call | solution.py:282
  58.3 1.3 %copy.6 = bf16[1,256,4096]{2,1,0:T(8,128)(2,1)} copy(bf16[1,256,4096]{2,1,0:T(8,128)(2,1)S(1)} %bitcast.3) | data formatting | bytes 4194304
Async XLA Ops:
  0.0 1.6 %copy-start = (bf16[1,256,4096]{2,1,0:T(8,128)(2,1)S(1)}, bf16[1,256,4096]{2,1,0:T(8,128)(2,1)}, u32[]{:S(2)}) copy-start(bf16[1,256,4096]{2,1,0:T(8,128)(2,1)} %param.4) | copy-start | bytes 6291460
  1.6 1.0 %copy-start.1 = (bf16[256,768]{1,0:T(8,128)(2,1)S(1)}, bf16[256,768]{1,0:T(8,128)(2,1)}, u32[]{:S(2)}) copy-start(bf16[256,768]{1,0:T(8,128)(2,1)} %w_ref.1) | copy-start | bytes 1179652
  2.6 0.9 %copy-start.2 = (bf16[256,256]{1,0:T(8,128)(2,1)S(1)}, bf16[256,256]{1,0:T(8,128)(2,1)}, u32[]{:S(2)}) copy-start(bf16[256,256]{1,0:T(8,128)(2,1)} %wo_ref.1) | copy-start | bytes 393220
  3.5 0.7 %copy-start.3 = (f32[256]{0:T(256)S(1)}, f32[256]{0:T(256)}, u32[]{:S(2)}) copy-start(f32[256]{0:T(256)} %param.6) | copy-start | bytes 3076

commit v2 on v1

v2 whole, which is shorter than its diff:
```python
import functools

import jax
import jax.numpy as jnp
from jax import lax
from jax.experimental import pallas as pl
from jax.experimental.pallas import tpu as pltpu
from jax.sharding import PartitionSpec as P

MESH = pl.DeviceIdType.MESH
BF16, F32 = jnp.bfloat16, jnp.float32
HEAD = 128
SIDE = 4
GROUP = 4
GROUPS = 4
TOK = 256
BLK = 256


def mod4(value):
    return lax.rem(value + 8, 4)


def kernel(
    tok_ref, w_ref, gain_ref, wo_ref, out_ref,
    x_buf, kv, q, wo, k_act, v_act, intra, near, far, total, nrm, nrm_out, out_buf, gain_buf,
    kv_acc, q_act, state,
    load_sem, send_sem, full_sem, half_sem, z_sem, scan_send, near_sem, far_sem, pair_send, pair_recv, wo_recv,
    store_sem, ready_sem,
):
    dp, seq = lax.axis_index("dp"), lax.axis_index("seq")
    y, x = lax.div(dp, SIDE), lax.rem(dp, SIDE)
    z, core = lax.div(seq, 2), lax.rem(seq, 2)
    grp, mem = lax.div(z, GROUP), lax.rem(z, GROUP)
    odd = lax.rem(z, 2)
    sibling = (dp, z * 2 + (1 - core))
    lane = pl.multiple_of(core * HEAD, HEAD)

    def at_xy(axis, off):
        if axis == 0:
            return (y * SIDE + mod4(x + off), seq)
        return (mod4(y + off) * SIDE + x, seq)

    def at_z(g, m):
        return (dp, (g * GROUP + m) * 2 + core)

    def along_z(off):
        return (dp, lax.rem(z + off + 16, 16) * 2 + core)

    own_tokens = x_buf.at[pl.ds(pl.multiple_of(core * TOK, TOK), TOK)]
    loads = [
        pltpu.make_async_copy(w_ref.at[:, pl.ds(2 * HEAD + lane, HEAD)], kv.at[dp, :, pl.ds(0, HEAD)], load_sem.at[0]),
        pltpu.make_async_copy(w_ref.at[:, pl.ds(4 * HEAD + lane, HEAD)], kv.at[dp, :, pl.ds(HEAD, HEAD)], load_sem.at[1]),
        pltpu.make_async_copy(w_ref.at[:, pl.ds(lane, HEAD)], q.at[dp], load_sem.at[2]),
        pltpu.make_async_copy(wo_ref.at[:, pl.ds(lane, HEAD)], wo.at[core, dp], load_sem.at[3]),
        pltpu.make_async_copy(tok_ref, own_tokens, load_sem.at[4]),
        pltpu.make_async_copy(gain_ref, gain_buf, load_sem.at[5]),
    ]
    for copy in loads:
        copy.start()
    far[...] = jnp.zeros_like(far)

    barrier = pltpu.get_barrier_semaphore()
    partners = [sibling]
    for off in (1, 2, 3):
        partners += [at_xy(0, off), at_xy(1, off)]
    for off in (1, 2, 3, 4):
        partners += [along_z(off), along_z(-off)]
    for partner in partners:
        pl.semaphore_signal(barrier, inc=1, device_id=partner, device_id_type=MESH)
    pl.semaphore_wait(barrier, len(partners))
    pl.semaphore_signal(ready_sem, inc=1, device_id=along_z(4), device_id_type=MESH)

    def piece(s, block, half, sub=None):
        if s == 0:
            rows = 96
            start = 160 * odd if half == 0 else 96 - 32 * odd
        else:
            rows = 128
            start = half * rows
        if sub is not None:
            start, rows = start + sub * (rows // 2), rows // 2
        start = pl.multiple_of(start, 16) if not isinstance(start, int) else start
        return (kv, q, wo.at[core])[s].at[block, pl.ds(start, rows)]

    def block_at(half, first, second):
        dy, dx = (second, first) if half == 0 else (first, second)
        return mod4(y + dy) * SIDE + mod4(x + dx)

    def send(ref, send_to, received, device):
        pltpu.make_async_remote_copy(
            src_ref=ref, dst_ref=ref, send_sem=send_to, recv_sem=received, device_id=device, device_id_type=MESH
        ).start()

    def wait(ref, sem):
        pltpu.make_async_copy(ref, ref, sem).wait()

    def send_full(s, half, block, axis, off):
        send(piece(s, block, half), send_sem.at[s], full_sem.at[s, half, block], at_xy(axis, off))

    def wait_full(s, half, block):
        wait(piece(s, block, half), full_sem.at[s, half, block])

    def send_half(s, half, block, sub, axis, off):
        send(piece(s, block, half, sub), send_sem.at[s], half_sem.at[s, half, block, sub], at_xy(axis, off))

    def wait_halves(s, half, block):
        for sub in (0, 1):
            wait(piece(s, block, half, sub), half_sem.at[s, half, block, sub])

    def z_rows(parity, block, part):
        return kv.at[block, pl.ds(pl.multiple_of(192 * parity + 32 * part, 32), 32)]

    def send_z(block):
        for part, off in ((0, 1), (1, -1)):
            send(z_rows(odd, block, part), send_sem.at[3], z_sem.at[block, part], along_z(off))

    def wait_z(block):
        for part in (0, 1):
            wait(z_rows(1 - odd, block, part), z_sem.at[block, part])

    def stage0(s):
        for half in (0, 1):
            for off in (1, -1):
                send_full(s, half, dp, half, off)
        if s == 0:
            for half in (0, 1):
                send_full(s, half, dp, half, 2)
        for half in (0, 1):
            for off in (1, -1):
                send_full(s, half, dp, 1 - half, off)

    def stage1(s):
        for first in (1, -1):
            for half in (0, 1):
                block = block_at(half, first, 0)
                wait_full(s, half, block)
                if s > 0:
                    send_half(s, half, block, 0 if first == -1 else 1, half, -first)
                for off in (1, -1):
                    send_full(s, half, block, 1 - half, off)
                if s == 0 and half == 0:
                    send_z(block)
        for half in (0, 1):
            block = block_at(half, 2, 0)
            if s == 0:
                wait_full(s, half, block)
            else:
                wait_halves(s, half, block)
            for off in (1, -1):
                send_full(s, half, block, 1 - half, off)
            if s == 0 and half == 0:
                send_z(block)

    def stage2(s):
        for first in (0, 1, -1, 2):
            for second in (-1, 1):
                for half in (0, 1):
                    block = block_at(half, first, second)
                    wait_full(s, half, block)
                    send_half(s, half, block, 0 if second == -1 else 1, 1 - half, -second)
                    if s == 0 and half == 0:
                        send_z(block)

    def sent(s):
        ref = (
            kv.at[pl.ds(0, 15), pl.ds(0, 192)],
            q.at[pl.ds(0, 15)],
            wo.at[0, pl.ds(0, 15)],
            kv.at[pl.ds(0, 15), pl.ds(0, 64)],
        )[s]
        wait(ref, send_sem.at[s])

    def project(weights, acc, part, first):
        wide = weights.shape[-1]
        term = jnp.dot(
            x_buf[:, pl.ds(pl.multiple_of(part * 1024, 1024), 1024)],
            weights[pl.ds(part * 4, 4)].reshape(1024, wide),
            preferred_element_type=F32,
        )
        if first:
            acc[...] = term
        else:
            acc[...] += term

    loads[0].wait()
    loads[1].wait()
    stage0(0)
    tokens_out = pltpu.make_async_remote_copy(
        src_ref=tok_ref, dst_ref=own_tokens,
        send_sem=pair_send.at[0], recv_sem=pair_recv.at[0], device_id=sibling, device_id_type=MESH,
    )
    tokens_out.start()
    stage1(0)
    stage2(0)
    loads[2].wait()
    stage0(1)
    for first in (0, 1, -1, 2):
        block = block_at(0, first, 2)
        wait_halves(0, 0, block)
        send_z(block)
    loads[3].wait()
    stage0(2)
    loads[4].wait()
    loads[5].wait()
    tokens_out.wait()

    for dy in (0, 1, -1, 2):
        wait_halves(0, 1, block_at(1, dy, 2))
        for dx in (0, 1, -1, 2):
            if (dy, dx) != (0, 0):
                wait_z(block_at(1, dy, dx))
        project(kv, kv_acc, mod4(y + dy), dy == 0)
    keys_in = kv_acc[:, :HEAD]
    k_act[...] = (keys_in / (1.0 + jnp.exp(-keys_in))).astype(BF16)
    v_act[...] = kv_acc[:, HEAD:].astype(BF16)
    for b in (0, 1):
        rows = pl.ds(b * TOK, TOK)
        state[b] = lax.dot_general(
            k_act[rows], v_act[rows], (((0,), (0,)), ((), ())), preferred_element_type=F32
        )
    near[mem] = (state[0] + state[1]).astype(BF16)

    for off in (1, 2, 3):
        send(near.at[mem], scan_send.at[off - 1], near_sem.at[mem], at_z(grp, mod4(mem + off)))
    stage1(1)
    stage1(2)
    for off in (1, 2, 3):
        m = mod4(mem + off)
        wait(near.at[m], near_sem.at[m])
    all_near = [near[m].astype(F32) for m in range(GROUP)]
    total[...] = (all_near[0] + all_near[1] + all_near[2] + all_near[3]).astype(BF16)

    pl.semaphore_wait(ready_sem, 1)
    for off in (2, 1, 3):
        g = grp + off

        @pl.when(g < GROUPS)
        def _():
            pltpu.make_async_remote_copy(
                src_ref=total, dst_ref=far.at[grp], send_sem=scan_send.at[2 + off], recv_sem=far_sem.at[grp],
                device_id=at_z(g, mem), device_id_type=MESH,
            ).start()

    prefix = jnp.zeros((HEAD, HEAD), F32)
    for m in range(GROUP - 1):
        prefix = prefix + jnp.where(m < mem, all_near[m], 0.0)

    def send_wo(block):
        send(wo.at[core, block], pair_send.at[1], wo_recv.at[block], sibling)

    inner = [(dy, dx) for dy in (0, 1, -1) for dx in (0, 1, -1)]
    outer = [(dy, 2) for dy in (0, 1, -1)] + [(2, dx) for dx in (0, 1, -1, 2)]
    stage2(1)
    stage2(2)
    for dy, dx in inner:
        send_wo(block_at(1, dy, dx))
    for half in (0, 1):
        for first in (0, 1, -1, 2):
            wait_halves(1, half, block_at(half, first, 2))
    for part in range(4):
        project(q, q_act, part, part == 0)
    queries = q_act[...]
    q_act[...] = queries / (1.0 + jnp.exp(-queries))
    causal = lax.broadcasted_iota(jnp.int32, (TOK, TOK), 0) >= lax.broadcasted_iota(jnp.int32, (TOK, TOK), 1)
    for b in (0, 1):
        rows = pl.ds(b * TOK, TOK)
        scores = lax.dot_general(
            q_act[rows].astype(BF16), k_act[rows], (((1,), (1,)), ((), ())), preferred_element_type=F32
        )
        scores = jnp.where(causal, scores, 0.0).astype(BF16)
        intra[rows] = jnp.dot(scores, v_act[rows], preferred_element_type=F32)
    for half in (0, 1):
        for first in (0, 1, -1, 2):
            wait_halves(2, half, block_at(half, first, 2))
    for dy, dx in outer:
        send_wo(block_at(1, dy, dx))
    for s in range(4):
        sent(s)
    for off in (1, 2, 3):
        wait(near.at[0], scan_send.at[off - 1])

    for g in range(GROUPS - 1):

        @pl.when(g < grp)
        def _():
            wait(far.at[g], far_sem.at[g])

        prefix = prefix + jnp.where(g < grp, far[g].astype(F32), 0.0)

    gain = gain_buf[pl.ds(core, 1), :]

    def normed(b):
        rows = pl.ds(pl.multiple_of(b * TOK, TOK), TOK)
        before = prefix + jnp.where(b == 1, state[0], 0.0)
        attended = intra[rows] + jnp.dot(
            q_act[rows].astype(BF16), before.astype(BF16), preferred_element_type=F32
        )
        meansq = jnp.mean(attended * attended, axis=-1, keepdims=True)
        return (attended * lax.rsqrt(meansq + 1e-06) * gain).astype(BF16)

    nrm_out[...] = normed(1 - core)
    nrm_copy = pltpu.make_async_remote_copy(
        src_ref=nrm_out, dst_ref=nrm.at[core], send_sem=pair_send.at[2], recv_sem=pair_recv.at[1],
        device_id=sibling, device_id_type=MESH,
    )
    nrm_copy.start()
    nrm[core] = normed(core)
    nrm_copy.wait()
    lhs = jnp.concatenate([nrm[0], nrm[1]], axis=1)
    stores = []
    for dy, dx in inner + outer:
        block = block_at(1, dy, dx)
        wait(wo.at[1 - core, block], wo_recv.at[block])
        columns = pl.ds(pl.multiple_of(block * BLK, BLK), BLK)
        weights = jnp.concatenate([wo[0, block], wo[1, block]], axis=1)
        out_buf[:, columns] = jnp.dot(lhs, weights, preferred_element_type=F32).astype(BF16)
        copy = pltpu.make_async_copy(out_buf.at[:, columns], out_ref.at[:, columns], store_sem.at[block])
        copy.start()
        stores.append(copy)
    wait(wo.at[core], pair_send.at[1])
    for off in (1, 2, 3):

        @pl.when(grp + off < GROUPS)
        def _():
            wait(total, scan_send.at[2 + off])

    for copy in stores:
        copy.wait()


def shards(tokens, w_qkv, norm_gain, w_out):
    hbm = pl.BlockSpec(memory_space=pl.ANY)
    dma = pltpu.SemaphoreType.DMA
    width = tokens.shape[2]
    out = pl.pallas_call(
        kernel,
        out_shape=jax.ShapeDtypeStruct((TOK, width), BF16),
        in_specs=[hbm] * 4,
        out_specs=hbm,
        scratch_shapes=[
            pltpu.VMEM((2 * TOK, width), BF16),
            pltpu.VMEM((16, BLK, 2 * HEAD), BF16),
            pltpu.VMEM((16, BLK, HEAD), BF16),
            pltpu.VMEM((2, 16, 2 * HEAD, BLK // 2), BF16),
            pltpu.VMEM((2 * TOK, HEAD), BF16),
            pltpu.VMEM((2 * TOK, HEAD), BF16),
            pltpu.VMEM((2 * TOK, HEAD), F32),
            pltpu.VMEM((GROUP, HEAD, HEAD), BF16),
            pltpu.VMEM((GROUPS, HEAD, HEAD), BF16),
            pltpu.VMEM((HEAD, HEAD), BF16),
            pltpu.VMEM((2, TOK, HEAD), BF16),
            pltpu.VMEM((TOK, HEAD), BF16),
            pltpu.VMEM((TOK, width), BF16),
            pltpu.VMEM((2, HEAD), F32),
            pltpu.VMEM((2 * TOK, 2 * HEAD), F32),
            pltpu.VMEM((2 * TOK, HEAD), F32),
            pltpu.VMEM((2, HEAD, HEAD), F32),
            dma((6,)),
            dma((4,)),
            dma((3, 2, 16)),
            dma((3, 2, 16, 2)),
            dma((16, 2)),
            dma((6,)),
            dma((GROUP,)),
            dma((GROUPS,)),
            dma((3,)),
            dma((2,)),
            dma((16,)),
            dma((16,)),
            pltpu.SemaphoreType.REGULAR,
        ],
        compiler_params=pltpu.CompilerParams(
            collective_id=0, has_side_effects=True, vmem_limit_bytes=48 * 1024 * 1024
        ),
        name="attention_layer",
    )(*(pltpu.with_memory_space_constraint(a, pltpu.HBM) for a in (tokens[0], w_qkv, norm_gain.reshape(2, HEAD), w_out)))
    return out[None]


def solution(mesh):
    return jax.shard_map(
        shards,
        mesh=mesh,
        in_specs=(P("dp", "seq", None), P("dp", None), P(), P(None, "dp")),
        out_specs=P("dp", "seq", None),
        check_vma=False,
    )
```

time: 59.8 us -> 58.9 us (0.985)
  local copies, waits for them, and re-layouts: 5.49 us -> 1.32 us
  Pallas kernels: 54.1 us -> 57.5 us
    unnamed x9 -> x1, local copies, waits for them, and re-layouts: 5.49 us -> 1.32 us
    pallas_call x1, Pallas kernels: 54.1 us -> 57.5 us  [shards(): pl.pallas_call(kernel, out_shape=jax.ShapeDtypeStruct((TOK, width), BF16)...]
where the time goes in v2:
time: 58.9 us; the launch traced here: 58.8 us
  Pallas kernels  57.5 us (98%)
  local copies, waits for them, and re-layouts  1.32 us (2%)
    pallas_call x1, Pallas kernels, shards(): pl.pallas_call(kernel, out_shape=jax.ShapeDtypeStruct((TOK, width), BF16)...  57.5 us
    unnamed x1, local copies, waits for them, and re-layouts  1.32 us

profile of v2, /device:TPU:1, one launch (start us, length us, event | category | flops | bytes accessed | tf_op | source)
XLA Modules:
  0.0 58.8 jit_solution(5287657895174049739)
XLA Ops:
  0.0 57.5 %attention_layer.1 = bf16[256,4096]{1,0:T(8,128)(2,1)S(1)} custom-call(bf16[256,4096]{1,0:T(8,128)(2,1)} %bitcast.4, bf16[256,768]{1,0:T(8,128)(2,1)} %w_ref.1, f32[2,128]{1,0:T(2,128)} %bitcast.5, bf16[256,256]{1,0:T(8,128)(2,1)} %wo_ref.1), custom_call_target="tpu_custom_call" | custom-call | tf_op jit(solution)/shard_map/attention_layer/pallas_call | solution.py:336
  57.5 1.3 %copy.6 = bf16[1,256,4096]{2,1,0:T(8,128)(2,1)} copy(bf16[1,256,4096]{2,1,0:T(8,128)(2,1)S(1)} %bitcast.3) | data formatting | bytes 4194304

commit v3 on v2

--- a/solution.py
+++ b/solution.py
@@ -23,7 +23,7 @@
 
 def kernel(
     tok_ref, w_ref, gain_ref, wo_ref, out_ref,
-    x_buf, kv, q, wo, k_act, v_act, intra, near, far, total, nrm, nrm_out, out_buf, gain_buf,
+    x_buf, kv, qo, wo_pair, k_act, v_act, intra, near, far, total, nrm, nrm_out, out_buf, gain_buf,
     kv_acc, q_act, state,
     load_sem, send_sem, full_sem, half_sem, z_sem, scan_send, near_sem, far_sem, pair_send, pair_recv, wo_recv,
     store_sem, ready_sem,
@@ -51,8 +51,8 @@
     loads = [
         pltpu.make_async_copy(w_ref.at[:, pl.ds(2 * HEAD + lane, HEAD)], kv.at[dp, :, pl.ds(0, HEAD)], load_sem.at[0]),
         pltpu.make_async_copy(w_ref.at[:, pl.ds(4 * HEAD + lane, HEAD)], kv.at[dp, :, pl.ds(HEAD, HEAD)], load_sem.at[1]),
-        pltpu.make_async_copy(w_ref.at[:, pl.ds(lane, HEAD)], q.at[dp], load_sem.at[2]),
-        pltpu.make_async_copy(wo_ref.at[:, pl.ds(lane, HEAD)], wo.at[core, dp], load_sem.at[3]),
+        pltpu.make_async_copy(w_ref.at[:, pl.ds(lane, HEAD)], qo.at[dp, 0], load_sem.at[2]),
+        pltpu.make_async_copy(wo_ref.at[:, pl.ds(lane, HEAD)], qo.at[dp, 1], load_sem.at[3]),
         pltpu.make_async_copy(tok_ref, own_tokens, load_sem.at[4]),
         pltpu.make_async_copy(gain_ref, gain_buf, load_sem.at[5]),
     ]
@@ -64,12 +64,17 @@
     partners = [sibling]
     for off in (1, 2, 3):
         partners += [at_xy(0, off), at_xy(1, off)]
-    for off in (1, 2, 3, 4):
-        partners += [along_z(off), along_z(-off)]
+    partners += [along_z(1), along_z(-1)]
     for partner in partners:
         pl.semaphore_signal(barrier, inc=1, device_id=partner, device_id_type=MESH)
     pl.semaphore_wait(barrier, len(partners))
-    pl.semaphore_signal(ready_sem, inc=1, device_id=along_z(4), device_id_type=MESH)
+
+    def tell(n):
+        for off in (2**n, -(2**n)):
+            pl.semaphore_signal(ready_sem.at[n], inc=1, device_id=along_z(off), device_id_type=MESH)
+
+    def hear(n):
+        pl.semaphore_wait(ready_sem.at[n], 2)
 
     def piece(s, block, half, sub=None):
         if s == 0:
@@ -81,7 +86,7 @@
         if sub is not None:
             start, rows = start + sub * (rows // 2), rows // 2
         start = pl.multiple_of(start, 16) if not isinstance(start, int) else start
-        return (kv, q, wo.at[core])[s].at[block, pl.ds(start, rows)]
+        return kv.at[block, pl.ds(start, rows)] if s == 0 else qo.at[block, :, pl.ds(start, rows)]
 
     def block_at(half, first, second):
         dy, dx = (second, first) if half == 0 else (first, second)
@@ -123,34 +128,21 @@
         for half in (0, 1):
             for off in (1, -1):
                 send_full(s, half, dp, half, off)
-        if s == 0:
-            for half in (0, 1):
-                send_full(s, half, dp, half, 2)
+        for half in (0, 1):
+            send_full(s, half, dp, half, 2)
         for half in (0, 1):
             for off in (1, -1):
                 send_full(s, half, dp, 1 - half, off)
 
     def stage1(s):
-        for first in (1, -1):
+        for first in (1, -1, 2):
             for half in (0, 1):
                 block = block_at(half, first, 0)
                 wait_full(s, half, block)
-                if s > 0:
-                    send_half(s, half, block, 0 if first == -1 else 1, half, -first)
                 for off in (1, -1):
                     send_full(s, half, block, 1 - half, off)
                 if s == 0 and half == 0:
                     send_z(block)
-        for half in (0, 1):
-            block = block_at(half, 2, 0)
-            if s == 0:
-                wait_full(s, half, block)
-            else:
-                wait_halves(s, half, block)
-            for off in (1, -1):
-                send_full(s, half, block, 1 - half, off)
-            if s == 0 and half == 0:
-                send_z(block)
 
     def stage2(s):
         for first in (0, 1, -1, 2):
@@ -163,20 +155,12 @@
                         send_z(block)
 
     def sent(s):
-        ref = (
-            kv.at[pl.ds(0, 15), pl.ds(0, 192)],
-            q.at[pl.ds(0, 15)],
-            wo.at[0, pl.ds(0, 15)],
-            kv.at[pl.ds(0, 15), pl.ds(0, 64)],
-        )[s]
+        ref = (kv.at[pl.ds(0, 15), pl.ds(0, 192)], qo.at[pl.ds(0, 15)], None, kv.at[pl.ds(0, 15), pl.ds(0, 64)])[s]
         wait(ref, send_sem.at[s])
 
     def project(weights, acc, part, first):
-        wide = weights.shape[-1]
         term = jnp.dot(
-            x_buf[:, pl.ds(pl.multiple_of(part * 1024, 1024), 1024)],
-            weights[pl.ds(part * 4, 4)].reshape(1024, wide),
-            preferred_element_type=F32,
+            x_buf[:, pl.ds(pl.multiple_of(part * 1024, 1024), 1024)], weights.reshape(1024, -1), preferred_element_type=F32
         )
         if first:
             acc[...] = term
@@ -191,16 +175,22 @@
         send_sem=pair_send.at[0], recv_sem=pair_recv.at[0], device_id=sibling, device_id_type=MESH,
     )
     tokens_out.start()
+    tell(0)
     stage1(0)
+    hear(0)
+    tell(1)
     stage2(0)
     loads[2].wait()
+    loads[3].wait()
     stage0(1)
+    hear(1)
+    tell(2)
     for first in (0, 1, -1, 2):
         block = block_at(0, first, 2)
         wait_halves(0, 0, block)
         send_z(block)
-    loads[3].wait()
-    stage0(2)
+    stage1(1)
+    hear(2)
     loads[4].wait()
     loads[5].wait()
     tokens_out.wait()
@@ -210,7 +200,8 @@
         for dx in (0, 1, -1, 2):
             if (dy, dx) != (0, 0):
                 wait_z(block_at(1, dy, dx))
-        project(kv, kv_acc, mod4(y + dy), dy == 0)
+        part = mod4(y + dy)
+        project(kv[pl.ds(part * 4, 4)], kv_acc, part, dy == 0)
     keys_in = kv_acc[:, :HEAD]
     k_act[...] = (keys_in / (1.0 + jnp.exp(-keys_in))).astype(BF16)
     v_act[...] = kv_acc[:, HEAD:].astype(BF16)
@@ -223,23 +214,25 @@
 
     for off in (1, 2, 3):
         send(near.at[mem], scan_send.at[off - 1], near_sem.at[mem], at_z(grp, mod4(mem + off)))
-    stage1(1)
-    stage1(2)
     for off in (1, 2, 3):
         m = mod4(mem + off)
         wait(near.at[m], near_sem.at[m])
     all_near = [near[m].astype(F32) for m in range(GROUP)]
     total[...] = (all_near[0] + all_near[1] + all_near[2] + all_near[3]).astype(BF16)
 
-    pl.semaphore_wait(ready_sem, 1)
-    for off in (2, 1, 3):
-        g = grp + off
-
-        @pl.when(g < GROUPS)
+    targets = [(2, 3, 0), (2, 0, 3), (2, 3, 1), (2, 0, 2), (1, None, None), (3, None, None)]
+
+    def sends_total(off, member):
+        inside = grp + off < GROUPS
+        return inside if member is None else jnp.logical_and(inside, mem == member)
+
+    for n, (off, member, target) in enumerate(targets):
+
+        @pl.when(sends_total(off, member))
         def _():
             pltpu.make_async_remote_copy(
-                src_ref=total, dst_ref=far.at[grp], send_sem=scan_send.at[2 + off], recv_sem=far_sem.at[grp],
-                device_id=at_z(g, mem), device_id_type=MESH,
+                src_ref=total, dst_ref=far.at[grp], send_sem=scan_send.at[3 + n], recv_sem=far_sem.at[grp],
+                device_id=at_z(grp + off, mem if target is None else target), device_id_type=MESH,
             ).start()
 
     prefix = jnp.zeros((HEAD, HEAD), F32)
@@ -247,19 +240,23 @@
         prefix = prefix + jnp.where(m < mem, all_near[m], 0.0)
 
     def send_wo(block):
-        send(wo.at[core, block], pair_send.at[1], wo_recv.at[block], sibling)
+        pltpu.make_async_remote_copy(
+            src_ref=qo.at[block, 1], dst_ref=wo_pair.at[block], send_sem=pair_send.at[1], recv_sem=wo_recv.at[block],
+            device_id=sibling, device_id_type=MESH,
+        ).start()
 
     inner = [(dy, dx) for dy in (0, 1, -1) for dx in (0, 1, -1)]
     outer = [(dy, 2) for dy in (0, 1, -1)] + [(2, dx) for dx in (0, 1, -1, 2)]
     stage2(1)
-    stage2(2)
     for dy, dx in inner:
         send_wo(block_at(1, dy, dx))
     for half in (0, 1):
         for first in (0, 1, -1, 2):
             wait_halves(1, half, block_at(half, first, 2))
+    for dy, dx in outer:
+        send_wo(block_at(1, dy, dx))
     for part in range(4):
-        project(q, q_act, part, part == 0)
+        project(qo[pl.ds(part * 4, 4), 0], q_act, part, part == 0)
     queries = q_act[...]
     q_act[...] = queries / (1.0 + jnp.exp(-queries))
     causal = lax.broadcasted_iota(jnp.int32, (TOK, TOK), 0) >= lax.broadcasted_iota(jnp.int32, (TOK, TOK), 1)
@@ -270,12 +267,7 @@
         )
         scores = jnp.where(causal, scores, 0.0).astype(BF16)
         intra[rows] = jnp.dot(scores, v_act[rows], preferred_element_type=F32)
-    for half in (0, 1):
-        for first in (0, 1, -1, 2):
-            wait_halves(2, half, block_at(half, first, 2))
-    for dy, dx in outer:
-        send_wo(block_at(1, dy, dx))
-    for s in range(4):
+    for s in (0, 1, 3):
         sent(s)
     for off in (1, 2, 3):
         wait(near.at[0], scan_send.at[off - 1])
@@ -311,19 +303,20 @@
     stores = []
     for dy, dx in inner + outer:
         block = block_at(1, dy, dx)
-        wait(wo.at[1 - core, block], wo_recv.at[block])
+        wait(wo_pair.at[block], wo_recv.at[block])
         columns = pl.ds(pl.multiple_of(block * BLK, BLK), BLK)
-        weights = jnp.concatenate([wo[0, block], wo[1, block]], axis=1)
+        own, other = qo[block, 1], wo_pair[block]
+        weights = jnp.concatenate([jnp.where(core == 0, own, other), jnp.where(core == 0, other, own)], axis=1)
         out_buf[:, columns] = jnp.dot(lhs, weights, preferred_element_type=F32).astype(BF16)
         copy = pltpu.make_async_copy(out_buf.at[:, columns], out_ref.at[:, columns], store_sem.at[block])
         copy.start()
         stores.append(copy)
-    wait(wo.at[core], pair_send.at[1])
-    for off in (1, 2, 3):
-
-        @pl.when(grp + off < GROUPS)
+    wait(wo_pair, pair_send.at[1])
+    for n, (off, member, _) in enumerate(targets):
+
+        @pl.when(sends_total(off, member))
         def _():
-            wait(total, scan_send.at[2 + off])
+            wait(total, scan_send.at[3 + n])
 
     for copy in stores:
         copy.wait()
@@ -341,8 +334,8 @@
         scratch_shapes=[
             pltpu.VMEM((2 * TOK, width), BF16),
             pltpu.VMEM((16, BLK, 2 * HEAD), BF16),
+            pltpu.VMEM((16, 2, BLK, HEAD), BF16),
             pltpu.VMEM((16, BLK, HEAD), BF16),
-            pltpu.VMEM((2, 16, 2 * HEAD, BLK // 2), BF16),
             pltpu.VMEM((2 * TOK, HEAD), BF16),
             pltpu.VMEM((2 * TOK, HEAD), BF16),
             pltpu.VMEM((2 * TOK, HEAD), F32),
@@ -358,17 +351,17 @@
             pltpu.VMEM((2, HEAD, HEAD), F32),
             dma((6,)),
             dma((4,)),
-            dma((3, 2, 16)),
-            dma((3, 2, 16, 2)),
+            dma((2, 2, 16)),
+            dma((2, 2, 16, 2)),
             dma((16, 2)),
-            dma((6,)),
+            dma((9,)),
             dma((GROUP,)),
             dma((GROUPS,)),
             dma((3,)),
             dma((2,)),
             dma((16,)),
             dma((16,)),
-            pltpu.SemaphoreType.REGULAR,
+            pltpu.SemaphoreType.REGULAR((3,)),
         ],
         compiler_params=pltpu.CompilerParams(
             collective_id=0, has_side_effects=True, vmem_limit_bytes=48 * 1024 * 1024

time: 58.9 us -> 51.1 us (0.87)
  Pallas kernels: 57.5 us -> 49.7 us
    pallas_call x1, Pallas kernels: 57.5 us -> 49.7 us  [shards(): pl.pallas_call(kernel, out_shape=jax.ShapeDtypeStruct((TOK, width), BF16)...]
where the time goes in v3:
time: 51.1 us; the launch traced here: 51 us
  Pallas kernels  49.7 us (97%)
  local copies, waits for them, and re-layouts  1.32 us (3%)
    pallas_call x1, Pallas kernels, shards(): pl.pallas_call(kernel, out_shape=jax.ShapeDtypeStruct((TOK, width), BF16)...  49.7 us
    unnamed x1, local copies, waits for them, and re-layouts  1.32 us

profile of v3, /device:TPU:1, one launch (start us, length us, event | category | flops | bytes accessed | tf_op | source)
XLA Modules:
  0.0 51.0 jit_solution(16042101355121575016)
XLA Ops:
  0.0 49.7 %attention_layer.1 = bf16[256,4096]{1,0:T(8,128)(2,1)S(1)} custom-call(bf16[256,4096]{1,0:T(8,128)(2,1)} %bitcast.4, bf16[256,768]{1,0:T(8,128)(2,1)} %w_ref.1, f32[2,128]{1,0:T(2,128)} %bitcast.5, bf16[256,256]{1,0:T(8,128)(2,1)} %wo_ref.1), custom_call_target="tpu_custom_call" | custom-call | tf_op jit(solution)/shard_map/attention_layer/pallas_call | solution.py:329
  49.7 1.3 %copy.6 = bf16[1,256,4096]{2,1,0:T(8,128)(2,1)} copy(bf16[1,256,4096]{2,1,0:T(8,128)(2,1)S(1)} %bitcast.3) | data formatting | bytes 4194304

commit v4 on v3

v4 whole, which is shorter than its diff:
```python
import functools

import jax
import jax.numpy as jnp
from jax import lax
from jax.experimental import pallas as pl
from jax.experimental.pallas import tpu as pltpu
from jax.sharding import PartitionSpec as P

MESH = pl.DeviceIdType.MESH
BF16, F32 = jnp.bfloat16, jnp.float32
HEAD = 128
SIDE = 4
GROUP = 4
GROUPS = 4
TOK = 256
BLK = 256


OFFSETS = (0, 1, -1, 2)


def slot_of(off):
    return OFFSETS.index(2 if off in (2, -2) else off)


def mod4(value):
    return lax.rem(value + 8, 4)


def kernel(
    tok_ref, w_ref, gain_ref, wo_ref, out_ref,
    x_buf, kv, qo, wo_pair, k_act, v_act, intra, near, far, total, nrm, nrm_out, out_buf, gain_buf,
    kv_acc, q_act, state,
    load_sem, send_sem, first_sem, second_sem, third_sem, scan_send, near_sem, far_sem, pair_send, pair_recv, wo_recv,
    store_sem, ready_sem,
):
    dp, seq = lax.axis_index("dp"), lax.axis_index("seq")
    y, x = lax.div(dp, SIDE), lax.rem(dp, SIDE)
    z, core = lax.div(seq, 2), lax.rem(seq, 2)
    grp, mem = lax.div(z, GROUP), lax.rem(z, GROUP)
    sibling = (dp, z * 2 + (1 - core))
    lane = pl.multiple_of(core * HEAD, HEAD)

    def at_xy(axis, off):
        if axis == 0:
            return (y * SIDE + mod4(x + off), seq)
        return (mod4(y + off) * SIDE + x, seq)

    def at_z(g, m):
        return (dp, (g * GROUP + m) * 2 + core)

    def along_z(off):
        return (dp, lax.rem(z + off + 16, 16) * 2 + core)

    own_tokens = x_buf.at[pl.ds(pl.multiple_of(core * TOK, TOK), TOK)]
    loads = [
        pltpu.make_async_copy(w_ref.at[:, pl.ds(2 * HEAD + lane, HEAD)], kv.at[0, 0, :, pl.ds(0, HEAD)], load_sem.at[0]),
        pltpu.make_async_copy(w_ref.at[:, pl.ds(4 * HEAD + lane, HEAD)], kv.at[0, 0, :, pl.ds(HEAD, HEAD)], load_sem.at[1]),
        pltpu.make_async_copy(w_ref.at[:, pl.ds(lane, HEAD)], qo.at[0, 0, 0], load_sem.at[2]),
        pltpu.make_async_copy(wo_ref.at[:, pl.ds(lane, HEAD)], qo.at[0, 0, 1], load_sem.at[3]),
        pltpu.make_async_copy(tok_ref, own_tokens, load_sem.at[4]),
        pltpu.make_async_copy(gain_ref, gain_buf, load_sem.at[5]),
    ]
    for copy in loads:
        copy.start()
    far[...] = jnp.zeros_like(far)

    barrier = pltpu.get_barrier_semaphore()
    partners = [sibling]
    for off in (1, 2, 3):
        partners += [at_xy(0, off), at_xy(1, off)]
    partners += [along_z(1), along_z(-1)]
    for partner in partners:
        pl.semaphore_signal(barrier, inc=1, device_id=partner, device_id_type=MESH)
    pl.semaphore_wait(barrier, len(partners))

    def tell(n):
        for off in (2**n, -(2**n)):
            pl.semaphore_signal(ready_sem.at[n], inc=1, device_id=along_z(off), device_id_type=MESH)

    def hear(n):
        pl.semaphore_wait(ready_sem.at[n], 2)

    def part_of(s, half, first, second, sub=None):
        rows = BLK // 2
        start = half * rows
        if sub is not None:
            start, rows = start + sub * (rows // 2), rows // 2
        at = (second, first) if half == 0 else (first, second)
        if s == 0:
            return kv.at[(*at, pl.ds(start, rows))]
        return qo.at[(*at, slice(None), pl.ds(start, rows))]

    rest = pl.ds(1, 3)

    def send(src, dst, send_to, received, device):
        pltpu.make_async_remote_copy(
            src_ref=src, dst_ref=dst, send_sem=send_to, recv_sem=received, device_id=device, device_id_type=MESH
        ).start()

    def wait(ref, sem):
        pltpu.make_async_copy(ref, ref, sem).wait()

    def start_first(s):
        for off in (1, -1, 2):
            for half in (0, 1):
                to = slot_of(-off)
                send(part_of(s, half, 0, 0), part_of(s, half, to, 0), send_sem.at[s], first_sem.at[s, half, to], at_xy(half, off))

    def start_second(s):
        for half in (0, 1):
            for off in (1, -1):
                to = slot_of(-off)
                send(part_of(s, half, 0, 0), part_of(s, half, 0, to), send_sem.at[s], second_sem.at[s, half, 0, to], at_xy(1 - half, off))

    def wait_first(s, half, first):
        wait(part_of(s, half, first, 0), first_sem.at[s, half, first])

    def pass_second(s, half, first, index):
        for off in (1, -1):
            to = slot_of(-off)
            send(
                part_of(s, half, first, 0), part_of(s, half, first, to), send_sem.at[s],
                second_sem.at[s, half, index, to], at_xy(1 - half, off),
            )

    def wait_second(s, half, first, index, second):
        wait(part_of(s, half, first, second), second_sem.at[s, half, index, second])

    def pass_third(s, half, first, index, second):
        sub = 0 if OFFSETS[second] == -1 else 1
        send(
            part_of(s, half, first, second, sub), part_of(s, half, first, 3, sub), send_sem.at[s],
            third_sem.at[s, half, index, sub], at_xy(1 - half, -OFFSETS[second]),
        )

    def wait_third(s, half, first, index):
        for sub in (0, 1):
            wait(part_of(s, half, first, 3, sub), third_sem.at[s, half, index, sub])

    def sent(s):
        rows = pl.ds(0, BLK * 15 // 16)
        wait(kv.at[:, :, rows] if s == 0 else qo.at[:, :, :, rows], send_sem.at[s])

    def block_at(a, b):
        return mod4(y + OFFSETS[a]) * SIDE + mod4(x + OFFSETS[b])

    def project(weights, acc, a):
        tokens = [x_buf[:, pl.ds(pl.multiple_of(block_at(a, b) * BLK, BLK), BLK)] for b in range(4)]
        term = jnp.dot(
            jnp.concatenate(tokens, axis=1), weights.reshape(SIDE * BLK, weights.shape[-1]), preferred_element_type=F32
        )
        if a == 0:
            acc[...] = term
        else:
            acc[...] += term

    loads[0].wait()
    loads[1].wait()
    start_first(0)
    start_second(0)
    tokens_out = pltpu.make_async_remote_copy(
        src_ref=tok_ref, dst_ref=own_tokens,
        send_sem=pair_send.at[0], recv_sem=pair_recv.at[0], device_id=sibling, device_id_type=MESH,
    )
    tokens_out.start()
    tell(0)
    for first in (1, 2, 3):
        for half in (0, 1):
            wait_first(0, half, first)
            pass_second(0, half, first, first)
    hear(0)
    tell(1)
    loads[2].wait()
    loads[3].wait()
    start_first(1)
    for half in (0, 1):
        for second in (1, 2):
            wait_second(0, half, 0, 0, second)
            pass_third(0, half, 0, 0, second)
    start_second(1)
    for half in (0, 1):
        for second in (1, 2):
            for first in (1, 2, 3):
                wait_second(0, half, first, first, second)
            pass_third(0, half, rest, 1, second)
    hear(1)
    tell(2)
    for half in (0, 1):
        for first in (1, 2, 3):
            wait_first(1, half, first)
        pass_second(1, half, rest, 1)
    hear(2)
    loads[4].wait()
    loads[5].wait()
    tokens_out.wait()

    for a in range(4):
        if a < 2:
            wait_third(0, 1, rest if a else 0, a)
        elif a == 3:
            wait_third(0, 0, 0, 0)
            wait_third(0, 0, rest, 1)
        project(kv[a], kv_acc, a)
    keys_in = kv_acc[:, :HEAD]
    k_act[...] = (keys_in / (1.0 + jnp.exp(-keys_in))).astype(BF16)
    v_act[...] = kv_acc[:, HEAD:].astype(BF16)
    for b in (0, 1):
        rows = pl.ds(b * TOK, TOK)
        state[b] = lax.dot_general(
            k_act[rows], v_act[rows], (((0,), (0,)), ((), ())), preferred_element_type=F32
        )
    near[mem] = (state[0] + state[1]).astype(BF16)

    for off in (1, 2, 3):
        send(near.at[mem], near.at[mem], scan_send.at[off - 1], near_sem.at[mem], at_z(grp, mod4(mem + off)))
    for half in (0, 1):
        for second in (1, 2):
            wait_second(1, half, 0, 0, second)
            wait_second(1, half, rest, 1, second)
            pass_third(1, half, pl.ds(0, 4), 0, second)

    def send_wo(n, rows, columns):
        send(qo.at[rows, columns, 1], wo_pair.at[rows, columns], pair_send.at[1 + n], wo_recv.at[n], sibling)

    inner = pl.ds(0, 3)
    shares = [(inner, inner), (inner, 3), (3, pl.ds(0, 4))]
    send_wo(0, *shares[0])
    for off in (1, 2, 3):
        m = mod4(mem + off)
        wait(near.at[m], near_sem.at[m])
    all_near = [near[m].astype(F32) for m in range(GROUP)]
    total[...] = (all_near[0] + all_near[1] + all_near[2] + all_near[3]).astype(BF16)

    targets = [(2, 3, 0), (2, 0, 3), (2, 3, 1), (2, 0, 2), (1, None, None), (3, None, None)]

    def sends_total(off, member):
        inside = grp + off < GROUPS
        return inside if member is None else jnp.logical_and(inside, mem == member)

    for n, (off, member, target) in enumerate(targets):

        @pl.when(sends_total(off, member))
        def _():
            pltpu.make_async_remote_copy(
                src_ref=total, dst_ref=far.at[grp], send_sem=scan_send.at[3 + n], recv_sem=far_sem.at[grp],
                device_id=at_z(grp + off, mem if target is None else target), device_id_type=MESH,
            ).start()

    prefix = jnp.zeros((HEAD, HEAD), F32)
    for m in range(GROUP - 1):
        prefix = prefix + jnp.where(m < mem, all_near[m], 0.0)

    for half in (0, 1):
        wait_third(1, half, pl.ds(0, 4), 0)
    for n in (1, 2):
        send_wo(n, *shares[n])
    for a in range(4):
        project(qo[a, :, 0], q_act, a)
    queries = q_act[...]
    q_act[...] = queries / (1.0 + jnp.exp(-queries))
    causal = lax.broadcasted_iota(jnp.int32, (TOK, TOK), 0) >= lax.broadcasted_iota(jnp.int32, (TOK, TOK), 1)
    for b in (0, 1):
        rows = pl.ds(b * TOK, TOK)
        scores = lax.dot_general(
            q_act[rows].astype(BF16), k_act[rows], (((1,), (1,)), ((), ())), preferred_element_type=F32
        )
        scores = jnp.where(causal, scores, 0.0).astype(BF16)
        intra[rows] = jnp.dot(scores, v_act[rows], preferred_element_type=F32)
    for s in (0, 1):
        sent(s)
    for off in (1, 2, 3):
        wait(near.at[0], scan_send.at[off - 1])

    for g in range(GROUPS - 1):

        @pl.when(g < grp)
        def _():
            wait(far.at[g], far_sem.at[g])

        prefix = prefix + jnp.where(g < grp, far[g].astype(F32), 0.0)

    gain = gain_buf[pl.ds(core, 1), :]

    def normed(b):
        rows = pl.ds(pl.multiple_of(b * TOK, TOK), TOK)
        before = prefix + jnp.where(b == 1, state[0], 0.0)
        attended = intra[rows] + jnp.dot(
            q_act[rows].astype(BF16), before.astype(BF16), preferred_element_type=F32
        )
        meansq = jnp.mean(attended * attended, axis=-1, keepdims=True)
        return (attended * lax.rsqrt(meansq + 1e-06) * gain).astype(BF16)

    nrm_out[...] = normed(1 - core)
    nrm_copy = pltpu.make_async_remote_copy(
        src_ref=nrm_out, dst_ref=nrm.at[core], send_sem=pair_send.at[4], recv_sem=pair_recv.at[1],
        device_id=sibling, device_id_type=MESH,
    )
    nrm_copy.start()
    nrm[core] = normed(core)
    nrm_copy.wait()
    lhs = jnp.concatenate([nrm[0], nrm[1]], axis=1)
    stores = []
    order = [(a, b) for a in range(3) for b in range(3)] + [(a, 3) for a in range(3)] + [(3, b) for b in range(4)]
    for n, (a, b) in enumerate(order):
        if n in (0, 9, 12):
            share = (0, 9, 12).index(n)
            wait(wo_pair.at[shares[share]], wo_recv.at[share])
        block = block_at(a, b)
        columns = pl.ds(pl.multiple_of(block * BLK, BLK), BLK)
        own, other = qo[a, b, 1], wo_pair[a, b]
        weights = jnp.concatenate([jnp.where(core == 0, own, other), jnp.where(core == 0, other, own)], axis=1)
        out_buf[:, columns] = jnp.dot(lhs, weights, preferred_element_type=F32).astype(BF16)
        copy = pltpu.make_async_copy(out_buf.at[:, columns], out_ref.at[:, columns], store_sem.at[n])
        copy.start()
        stores.append(copy)
    for n, share in enumerate(shares):
        wait(wo_pair.at[share], pair_send.at[1 + n])
    for n, (off, member, _) in enumerate(targets):

        @pl.when(sends_total(off, member))
        def _():
            wait(total, scan_send.at[3 + n])

    for copy in stores:
        copy.wait()


def shards(tokens, w_qkv, norm_gain, w_out):
    hbm = pl.BlockSpec(memory_space=pl.ANY)
    dma = pltpu.SemaphoreType.DMA
    width = tokens.shape[2]
    out = pl.pallas_call(
        kernel,
        out_shape=jax.ShapeDtypeStruct((TOK, width), BF16),
        in_specs=[hbm] * 4,
        out_specs=hbm,
        scratch_shapes=[
            pltpu.VMEM((2 * TOK, width), BF16),
            pltpu.VMEM((SIDE, SIDE, BLK, 2 * HEAD), BF16),
            pltpu.VMEM((SIDE, SIDE, 2, BLK, HEAD), BF16),
            pltpu.VMEM((SIDE, SIDE, BLK, HEAD), BF16),
            pltpu.VMEM((2 * TOK, HEAD), BF16),
            pltpu.VMEM((2 * TOK, HEAD), BF16),
            pltpu.VMEM((2 * TOK, HEAD), F32),
            pltpu.VMEM((GROUP, HEAD, HEAD), BF16),
            pltpu.VMEM((GROUPS, HEAD, HEAD), BF16),
            pltpu.VMEM((HEAD, HEAD), BF16),
            pltpu.VMEM((2, TOK, HEAD), BF16),
            pltpu.VMEM((TOK, HEAD), BF16),
            pltpu.VMEM((TOK, width), BF16),
            pltpu.VMEM((2, HEAD), F32),
            pltpu.VMEM((2 * TOK, 2 * HEAD), F32),
            pltpu.VMEM((2 * TOK, HEAD), F32),
            pltpu.VMEM((2, HEAD, HEAD), F32),
            dma((6,)),
            dma((2,)),
            dma((2, 2, 4)),
            dma((2, 2, 4, 3)),
            dma((2, 2, 2, 2)),
            dma((9,)),
            dma((GROUP,)),
            dma((GROUPS,)),
            dma((5,)),
            dma((2,)),
            dma((3,)),
            dma((16,)),
            pltpu.SemaphoreType.REGULAR((3,)),
        ],
        compiler_params=pltpu.CompilerParams(
            collective_id=0, has_side_effects=True, vmem_limit_bytes=48 * 1024 * 1024
        ),
        name="attention_layer",
    )(*(pltpu.with_memory_space_constraint(a, pltpu.HBM) for a in (tokens[0], w_qkv, norm_gain.reshape(2, HEAD), w_out)))
    return out[None]


def solution(mesh):
    return jax.shard_map(
        shards,
        mesh=mesh,
        in_specs=(P("dp", "seq", None), P("dp", None), P(), P(None, "dp")),
        out_specs=P("dp", "seq", None),
        check_vma=False,
    )
```

time: 51.1 us -> 50.8 us (level)
  no operation moved by 1% of the time
where the time goes in v4:
time: 50.8 us; the launch traced here: 50.7 us
  Pallas kernels  49.4 us (97%)
  local copies, waits for them, and re-layouts  1.32 us (3%)
    pallas_call x1, Pallas kernels, shards(): pl.pallas_call(kernel, out_shape=jax.ShapeDtypeStruct((TOK, width), BF16)...  49.4 us
    unnamed x1, local copies, waits for them, and re-layouts  1.32 us

profile of v4, /device:TPU:1, one launch (start us, length us, event | category | flops | bytes accessed | tf_op | source)
XLA Modules:
  0.0 50.7 jit_solution(4563907310016269680)
XLA Ops:
  0.0 49.4 %attention_layer.1 = bf16[256,4096]{1,0:T(8,128)(2,1)S(1)} custom-call(bf16[256,4096]{1,0:T(8,128)(2,1)} %bitcast.4, bf16[256,768]{1,0:T(8,128)(2,1)} %w_ref.1, f32[2,128]{1,0:T(2,128)} %bitcast.5, bf16[256,256]{1,0:T(8,128)(2,1)} %wo_ref.1), custom_call_target="tpu_custom_call" | custom-call | tf_op jit(solution)/shard_map/attention_layer/pallas_call | solution.py:334
  49.4 1.3 %copy.6 = bf16[1,256,4096]{2,1,0:T(8,128)(2,1)} copy(bf16[1,256,4096]{2,1,0:T(8,128)(2,1)S(1)} %bitcast.3) | data formatting | bytes 4194304

commit v5 on v4

--- a/solution.py
+++ b/solution.py
@@ -90,7 +90,7 @@
         at = (second, first) if half == 0 else (first, second)
         if s == 0:
             return kv.at[(*at, pl.ds(start, rows))]
-        return qo.at[(*at, slice(None), pl.ds(start, rows))]
+        return qo.at[(*at, s - 1, pl.ds(start, rows))]
 
     rest = pl.ds(1, 3)
 
@@ -139,9 +139,22 @@
         for sub in (0, 1):
             wait(part_of(s, half, first, 3, sub), third_sem.at[s, half, index, sub])
 
+    def pass_seconds(s):
+        for half in (0, 1):
+            for first in (1, 2, 3):
+                wait_first(s, half, first)
+            pass_second(s, half, rest, 1)
+
+    def pass_thirds(s):
+        for half in (0, 1):
+            for second in (1, 2):
+                wait_second(s, half, 0, 0, second)
+                wait_second(s, half, rest, 1, second)
+                pass_third(s, half, pl.ds(0, 4), 0, second)
+
     def sent(s):
         rows = pl.ds(0, BLK * 15 // 16)
-        wait(kv.at[:, :, rows] if s == 0 else qo.at[:, :, :, rows], send_sem.at[s])
+        wait(kv.at[:, :, rows] if s == 0 else qo.at[:, :, 0, rows], send_sem.at[s])
 
     def block_at(a, b):
         return mod4(y + OFFSETS[a]) * SIDE + mod4(x + OFFSETS[b])
@@ -187,10 +200,9 @@
             pass_third(0, half, rest, 1, second)
     hear(1)
     tell(2)
-    for half in (0, 1):
-        for first in (1, 2, 3):
-            wait_first(1, half, first)
-        pass_second(1, half, rest, 1)
+    pass_seconds(1)
+    start_first(2)
+    start_second(2)
     hear(2)
     loads[4].wait()
     loads[5].wait()
@@ -215,18 +227,14 @@
 
     for off in (1, 2, 3):
         send(near.at[mem], near.at[mem], scan_send.at[off - 1], near_sem.at[mem], at_z(grp, mod4(mem + off)))
-    for half in (0, 1):
-        for second in (1, 2):
-            wait_second(1, half, 0, 0, second)
-            wait_second(1, half, rest, 1, second)
-            pass_third(1, half, pl.ds(0, 4), 0, second)
+    pass_thirds(1)
+    pass_seconds(2)
 
     def send_wo(n, rows, columns):
         send(qo.at[rows, columns, 1], wo_pair.at[rows, columns], pair_send.at[1 + n], wo_recv.at[n], sibling)
 
     inner = pl.ds(0, 3)
     shares = [(inner, inner), (inner, 3), (3, pl.ds(0, 4))]
-    send_wo(0, *shares[0])
     for off in (1, 2, 3):
         m = mod4(mem + off)
         wait(near.at[m], near_sem.at[m])
@@ -254,10 +262,10 @@
 
     for half in (0, 1):
         wait_third(1, half, pl.ds(0, 4), 0)
-    for n in (1, 2):
-        send_wo(n, *shares[n])
     for a in range(4):
         project(qo[a, :, 0], q_act, a)
+    pass_thirds(2)
+    send_wo(0, *shares[0])
     queries = q_act[...]
     q_act[...] = queries / (1.0 + jnp.exp(-queries))
     causal = lax.broadcasted_iota(jnp.int32, (TOK, TOK), 0) >= lax.broadcasted_iota(jnp.int32, (TOK, TOK), 1)
@@ -268,11 +276,6 @@
         )
         scores = jnp.where(causal, scores, 0.0).astype(BF16)
         intra[rows] = jnp.dot(scores, v_act[rows], preferred_element_type=F32)
-    for s in (0, 1):
-        sent(s)
-    for off in (1, 2, 3):
-        wait(near.at[0], scan_send.at[off - 1])
-
     for g in range(GROUPS - 1):
 
         @pl.when(g < grp)
@@ -299,6 +302,10 @@
     )
     nrm_copy.start()
     nrm[core] = normed(core)
+    for half in (0, 1):
+        wait_third(2, half, pl.ds(0, 4), 0)
+    for n in (1, 2):
+        send_wo(n, *shares[n])
     nrm_copy.wait()
     lhs = jnp.concatenate([nrm[0], nrm[1]], axis=1)
     stores = []
@@ -315,6 +322,10 @@
         copy = pltpu.make_async_copy(out_buf.at[:, columns], out_ref.at[:, columns], store_sem.at[n])
         copy.start()
         stores.append(copy)
+    for s in range(3):
+        sent(s)
+    for off in (1, 2, 3):
+        wait(near.at[0], scan_send.at[off - 1])
     for n, share in enumerate(shares):
         wait(wo_pair.at[share], pair_send.at[1 + n])
     for n, (off, member, _) in enumerate(targets):
@@ -355,10 +366,10 @@
             pltpu.VMEM((2 * TOK, HEAD), F32),
             pltpu.VMEM((2, HEAD, HEAD), F32),
             dma((6,)),
-            dma((2,)),
-            dma((2, 2, 4)),
-            dma((2, 2, 4, 3)),
-            dma((2, 2, 2, 2)),
+            dma((3,)),
+            dma((3, 2, 4)),
+            dma((3, 2, 4, 3)),
+            dma((3, 2, 2, 2)),
             dma((9,)),
             dma((GROUP,)),
             dma((GROUPS,)),

time: 50.8 us -> 48.8 us (0.961)
  Pallas kernels: 49.4 us -> 47.4 us
    pallas_call x1, Pallas kernels: 49.4 us -> 47.4 us  [shards(): pl.pallas_call(kernel, out_shape=jax.ShapeDtypeStruct((TOK, width), BF16)...]
where the time goes in v5:
time: 48.8 us; the launch traced here: 48.7 us
  Pallas kernels  47.4 us (97%)
  local copies, waits for them, and re-layouts  1.32 us (3%)
    pallas_call x1, Pallas kernels, shards(): pl.pallas_call(kernel, out_shape=jax.ShapeDtypeStruct((TOK, width), BF16)...  47.4 us
    unnamed x1, local copies, waits for them, and re-layouts  1.32 us

profile of v5, /device:TPU:1, one launch (start us, length us, event | category | flops | bytes accessed | tf_op | source)
XLA Modules:
  0.0 48.7 jit_solution(11828332869979802858)
XLA Ops:
  0.0 47.4 %attention_layer.1 = bf16[256,4096]{1,0:T(8,128)(2,1)S(1)} custom-call(bf16[256,4096]{1,0:T(8,128)(2,1)} %bitcast.4, bf16[256,768]{1,0:T(8,128)(2,1)} %w_ref.1, f32[2,128]{1,0:T(2,128)} %bitcast.5, bf16[256,256]{1,0:T(8,128)(2,1)} %wo_ref.1), custom_call_target="tpu_custom_call" | custom-call | tf_op jit(solution)/shard_map/attention_layer/pallas_call | solution.py:345
  47.4 1.3 %copy.6 = bf16[1,256,4096]{2,1,0:T(8,128)(2,1)} copy(bf16[1,256,4096]{2,1,0:T(8,128)(2,1)S(1)} %bitcast.3) | data formatting | bytes 4194304

commit v6 on v5

--- a/solution.py
+++ b/solution.py
@@ -30,10 +30,10 @@
 
 def kernel(
     tok_ref, w_ref, gain_ref, wo_ref, out_ref,
-    x_buf, kv, qo, wo_pair, k_act, v_act, intra, near, far, total, nrm, nrm_out, out_buf, gain_buf,
+    x_buf, kv, qo, wo_pair, k_act, v_act, intra, near, far, total, nrm, nrm_out, gain_buf,
     kv_acc, q_act, state,
     load_sem, send_sem, first_sem, second_sem, third_sem, scan_send, near_sem, far_sem, pair_send, pair_recv, wo_recv,
-    store_sem, ready_sem,
+    ready_sem,
 ):
     dp, seq = lax.axis_index("dp"), lax.axis_index("seq")
     y, x = lax.div(dp, SIDE), lax.rem(dp, SIDE)
@@ -102,6 +102,9 @@
     def wait(ref, sem):
         pltpu.make_async_copy(ref, ref, sem).wait()
 
+    def around(s):
+        return (2, 1, -1) if s == 2 else (1, -1)
+
     def start_first(s):
         for off in (1, -1, 2):
             for half in (0, 1):
@@ -110,7 +113,7 @@
 
     def start_second(s):
         for half in (0, 1):
-            for off in (1, -1):
+            for off in around(s):
                 to = slot_of(-off)
                 send(part_of(s, half, 0, 0), part_of(s, half, 0, to), send_sem.at[s], second_sem.at[s, half, 0, to], at_xy(1 - half, off))
 
@@ -118,7 +121,7 @@
         wait(part_of(s, half, first, 0), first_sem.at[s, half, first])
 
     def pass_second(s, half, first, index):
-        for off in (1, -1):
+        for off in around(s):
             to = slot_of(-off)
             send(
                 part_of(s, half, first, 0), part_of(s, half, first, to), send_sem.at[s],
@@ -159,15 +162,12 @@
     def block_at(a, b):
         return mod4(y + OFFSETS[a]) * SIDE + mod4(x + OFFSETS[b])
 
-    def project(weights, acc, a):
-        tokens = [x_buf[:, pl.ds(pl.multiple_of(block_at(a, b) * BLK, BLK), BLK)] for b in range(4)]
+    def project(weights, acc, slots, add):
+        tokens = [x_buf[:, pl.ds(pl.multiple_of(block_at(a, b) * BLK, BLK), BLK)] for a, b in slots]
         term = jnp.dot(
-            jnp.concatenate(tokens, axis=1), weights.reshape(SIDE * BLK, weights.shape[-1]), preferred_element_type=F32
-        )
-        if a == 0:
-            acc[...] = term
-        else:
-            acc[...] += term
+            jnp.concatenate(tokens, axis=1), weights.reshape(len(slots) * BLK, weights.shape[-1]), preferred_element_type=F32
+        )
+        acc[...] = acc[...] + term if add else term
 
     loads[0].wait()
     loads[1].wait()
@@ -208,13 +208,14 @@
     loads[5].wait()
     tokens_out.wait()
 
-    for a in range(4):
-        if a < 2:
-            wait_third(0, 1, rest if a else 0, a)
-        elif a == 3:
-            wait_third(0, 0, 0, 0)
-            wait_third(0, 0, rest, 1)
-        project(kv[a], kv_acc, a)
+    for a in range(3):
+        project(kv[a, 0:3], kv_acc, [(a, b) for b in range(3)], a > 0)
+    wait_third(0, 1, 0, 0)
+    wait_third(0, 1, rest, 1)
+    project(kv[0:3, 3], kv_acc, [(a, 3) for a in range(3)], True)
+    wait_third(0, 0, 0, 0)
+    wait_third(0, 0, rest, 1)
+    project(kv[3], kv_acc, [(3, b) for b in range(4)], True)
     keys_in = kv_acc[:, :HEAD]
     k_act[...] = (keys_in / (1.0 + jnp.exp(-keys_in))).astype(BF16)
     v_act[...] = kv_acc[:, HEAD:].astype(BF16)
@@ -263,8 +264,11 @@
     for half in (0, 1):
         wait_third(1, half, pl.ds(0, 4), 0)
     for a in range(4):
-        project(qo[a, :, 0], q_act, a)
-    pass_thirds(2)
+        project(qo[a, :, 0], q_act, [(a, b) for b in range(4)], a > 0)
+    for half in (0, 1):
+        for second in (1, 2):
+            wait_second(2, half, 0, 0, second)
+            wait_second(2, half, rest, 1, second)
     send_wo(0, *shares[0])
     queries = q_act[...]
     q_act[...] = queries / (1.0 + jnp.exp(-queries))
@@ -303,12 +307,12 @@
     nrm_copy.start()
     nrm[core] = normed(core)
     for half in (0, 1):
-        wait_third(2, half, pl.ds(0, 4), 0)
+        wait_second(2, half, 0, 0, 3)
+        wait_second(2, half, rest, 1, 3)
     for n in (1, 2):
         send_wo(n, *shares[n])
     nrm_copy.wait()
     lhs = jnp.concatenate([nrm[0], nrm[1]], axis=1)
-    stores = []
     order = [(a, b) for a in range(3) for b in range(3)] + [(a, 3) for a in range(3)] + [(3, b) for b in range(4)]
     for n, (a, b) in enumerate(order):
         if n in (0, 9, 12):
@@ -318,10 +322,7 @@
         columns = pl.ds(pl.multiple_of(block * BLK, BLK), BLK)
         own, other = qo[a, b, 1], wo_pair[a, b]
         weights = jnp.concatenate([jnp.where(core == 0, own, other), jnp.where(core == 0, other, own)], axis=1)
-        out_buf[:, columns] = jnp.dot(lhs, weights, preferred_element_type=F32).astype(BF16)
-        copy = pltpu.make_async_copy(out_buf.at[:, columns], out_ref.at[:, columns], store_sem.at[n])
-        copy.start()
-        stores.append(copy)
+        out_ref[:, columns] = jnp.dot(lhs, weights, preferred_element_type=F32).astype(BF16)
     for s in range(3):
         sent(s)
     for off in (1, 2, 3):
@@ -333,9 +334,6 @@
         @pl.when(sends_total(off, member))
         def _():
             wait(total, scan_send.at[3 + n])
-
-    for copy in stores:
-        copy.wait()
 
 
 def shards(tokens, w_qkv, norm_gain, w_out):
@@ -346,7 +344,7 @@
         kernel,
         out_shape=jax.ShapeDtypeStruct((TOK, width), BF16),
         in_specs=[hbm] * 4,
-        out_specs=hbm,
+        out_specs=pl.BlockSpec(memory_space=pltpu.VMEM),
         scratch_shapes=[
             pltpu.VMEM((2 * TOK, width), BF16),
             pltpu.VMEM((SIDE, SIDE, BLK, 2 * HEAD), BF16),
@@ -360,7 +358,6 @@
             pltpu.VMEM((HEAD, HEAD), BF16),
             pltpu.VMEM((2, TOK, HEAD), BF16),
             pltpu.VMEM((TOK, HEAD), BF16),
-            pltpu.VMEM((TOK, width), BF16),
             pltpu.VMEM((2, HEAD), F32),
             pltpu.VMEM((2 * TOK, 2 * HEAD), F32),
             pltpu.VMEM((2 * TOK, HEAD), F32),
@@ -368,7 +365,7 @@
             dma((6,)),
             dma((3,)),
             dma((3, 2, 4)),
-            dma((3, 2, 4, 3)),
+            dma((3, 2, 4, 4)),
             dma((3, 2, 2, 2)),
             dma((9,)),
             dma((GROUP,)),
@@ -376,7 +373,6 @@
             dma((5,)),
             dma((2,)),
             dma((3,)),
-            dma((16,)),
             pltpu.SemaphoreType.REGULAR((3,)),
         ],
         compiler_params=pltpu.CompilerParams(

time: 48.8 us -> 45.8 us (0.939)
  Pallas kernels: 47.4 us -> 44.4 us
    pallas_call x1, Pallas kernels: 47.4 us -> 44.4 us  [shards(): pl.pallas_call(kernel, out_shape=jax.ShapeDtypeStruct((TOK, width), BF16)...]
where the time goes in v6:
time: 45.8 us; the launch traced here: 45.7 us
  Pallas kernels  44.4 us (97%)
  local copies, waits for them, and re-layouts  1.32 us (3%)
    pallas_call x1, Pallas kernels, shards(): pl.pallas_call(kernel, out_shape=jax.ShapeDtypeStruct((TOK, width), BF16)...  44.4 us
    unnamed x1, local copies, waits for them, and re-layouts  1.32 us

profile of v6, /device:TPU:1, one launch (start us, length us, event | category | flops | bytes accessed | tf_op | source)
XLA Modules:
  0.0 45.7 jit_solution(3931099247117637830)
XLA Ops:
  0.0 44.4 %attention_layer.1 = bf16[256,4096]{1,0:T(8,128)(2,1)S(1)} custom-call(bf16[256,4096]{1,0:T(8,128)(2,1)} %bitcast.4, bf16[256,768]{1,0:T(8,128)(2,1)} %w_ref.1, f32[2,128]{1,0:T(2,128)} %bitcast.5, bf16[256,256]{1,0:T(8,128)(2,1)} %wo_ref.1), custom_call_target="tpu_custom_call" | custom-call | tf_op jit(solution)/shard_map/attention_layer/pallas_call | solution.py:343
  44.4 1.3 %copy.6 = bf16[1,256,4096]{2,1,0:T(8,128)(2,1)} copy(bf16[1,256,4096]{2,1,0:T(8,128)(2,1)S(1)} %bitcast.3) | data formatting | bytes 4194304

commit v7 on v6

--- a/solution.py
+++ b/solution.py
@@ -265,11 +265,6 @@
         wait_third(1, half, pl.ds(0, 4), 0)
     for a in range(4):
         project(qo[a, :, 0], q_act, [(a, b) for b in range(4)], a > 0)
-    for half in (0, 1):
-        for second in (1, 2):
-            wait_second(2, half, 0, 0, second)
-            wait_second(2, half, rest, 1, second)
-    send_wo(0, *shares[0])
     queries = q_act[...]
     q_act[...] = queries / (1.0 + jnp.exp(-queries))
     causal = lax.broadcasted_iota(jnp.int32, (TOK, TOK), 0) >= lax.broadcasted_iota(jnp.int32, (TOK, TOK), 1)
@@ -280,6 +275,11 @@
         )
         scores = jnp.where(causal, scores, 0.0).astype(BF16)
         intra[rows] = jnp.dot(scores, v_act[rows], preferred_element_type=F32)
+    for half in (0, 1):
+        for second in (1, 2):
+            wait_second(2, half, 0, 0, second)
+            wait_second(2, half, rest, 1, second)
+    send_wo(0, *shares[0])
     for g in range(GROUPS - 1):
 
         @pl.when(g < grp)

time: 45.8 us -> 45.8 us (level)
  no operation moved by 1% of the time
where the time goes in v7:
time: 45.8 us; the launch traced here: 45.7 us
  Pallas kernels  44.4 us (97%)
  local copies, waits for them, and re-layouts  1.32 us (3%)
    pallas_call x1, Pallas kernels, shards(): pl.pallas_call(kernel, out_shape=jax.ShapeDtypeStruct((TOK, width), BF16)...  44.4 us
    unnamed x1, local copies, waits for them, and re-layouts  1.32 us

profile of v7, /device:TPU:1, one launch (start us, length us, event | category | flops | bytes accessed | tf_op | source)
XLA Modules:
  0.0 45.7 jit_solution(16355964951362394557)
XLA Ops:
  0.0 44.4 %attention_layer.1 = bf16[256,4096]{1,0:T(8,128)(2,1)S(1)} custom-call(bf16[256,4096]{1,0:T(8,128)(2,1)} %bitcast.4, bf16[256,768]{1,0:T(8,128)(2,1)} %w_ref.1, f32[2,128]{1,0:T(2,128)} %bitcast.5, bf16[256,256]{1,0:T(8,128)(2,1)} %wo_ref.1), custom_call_target="tpu_custom_call" | custom-call | tf_op jit(solution)/shard_map/attention_layer/pallas_call | solution.py:343
  44.4 1.3 %copy.6 = bf16[1,256,4096]{2,1,0:T(8,128)(2,1)} copy(bf16[1,256,4096]{2,1,0:T(8,128)(2,1)S(1)} %bitcast.3) | data formatting | bytes 4194304

commit v8 on v7

--- a/solution.py
+++ b/solution.py
@@ -62,7 +62,7 @@
         pltpu.make_async_copy(tok_ref, own_tokens, load_sem.at[4]),
         pltpu.make_async_copy(gain_ref, gain_buf, load_sem.at[5]),
     ]
-    for copy in loads:
+    for copy in loads[:4] + loads[5:]:
         copy.start()
     far[...] = jnp.zeros_like(far)
 
@@ -177,6 +177,7 @@
         src_ref=tok_ref, dst_ref=own_tokens,
         send_sem=pair_send.at[0], recv_sem=pair_recv.at[0], device_id=sibling, device_id_type=MESH,
     )
+    loads[4].start()
     tokens_out.start()
     tell(0)
     for first in (1, 2, 3):
@@ -216,6 +217,7 @@
     wait_third(0, 0, 0, 0)
     wait_third(0, 0, rest, 1)
     project(kv[3], kv_acc, [(3, b) for b in range(4)], True)
+    pass_thirds(1)
     keys_in = kv_acc[:, :HEAD]
     k_act[...] = (keys_in / (1.0 + jnp.exp(-keys_in))).astype(BF16)
     v_act[...] = kv_acc[:, HEAD:].astype(BF16)
@@ -228,7 +230,6 @@
 
     for off in (1, 2, 3):
         send(near.at[mem], near.at[mem], scan_send.at[off - 1], near_sem.at[mem], at_z(grp, mod4(mem + off)))
-    pass_thirds(1)
     pass_seconds(2)
 
     def send_wo(n, rows, columns):

time: 45.8 us -> 45.8 us (level)
  no operation moved by 1% of the time
where the time goes in v8:
time: 45.8 us; the launch traced here: 45.7 us
  Pallas kernels  44.4 us (97%)
  local copies, waits for them, and re-layouts  1.32 us (3%)
    pallas_call x1, Pallas kernels, shards(): pl.pallas_call(kernel, out_shape=jax.ShapeDtypeStruct((TOK, width), BF16)...  44.4 us
    unnamed x1, local copies, waits for them, and re-layouts  1.32 us

profile of v8, /device:TPU:1, one launch (start us, length us, event | category | flops | bytes accessed | tf_op | source)
XLA Modules:
  0.0 45.7 jit_solution(9461561889238914353)
XLA Ops:
  0.0 44.4 %attention_layer.1 = bf16[256,4096]{1,0:T(8,128)(2,1)S(1)} custom-call(bf16[256,4096]{1,0:T(8,128)(2,1)} %bitcast.4, bf16[256,768]{1,0:T(8,128)(2,1)} %w_ref.1, f32[2,128]{1,0:T(2,128)} %bitcast.5, bf16[256,256]{1,0:T(8,128)(2,1)} %wo_ref.1), custom_call_target="tpu_custom_call" | custom-call | tf_op jit(solution)/shard_map/attention_layer/pallas_call | solution.py:344
  44.4 1.3 %copy.6 = bf16[1,256,4096]{2,1,0:T(8,128)(2,1)} copy(bf16[1,256,4096]{2,1,0:T(8,128)(2,1)S(1)} %bitcast.3) | data formatting | bytes 4194304
